TPU v7x, 32 devices: a whole 2x2x4 slice. The times are simulated.
32 devices in a mesh: seq: 4 (over z), mp: 8 (over y, x, core).
Axes of the slice: x: 2, y: 2, z: 4, core: 2. Of those that a mesh axis runs over, the one named last changes fastest.
Arguments:
- ids: int32 [16, 1024], P('seq'), may hold values from 0 to 274
- lengths: int32 [1024], replicated, may hold values from 1 to 16, 12288 in all
- order: int32 [1024], replicated, may hold values from 0 to 1023, each once
- h_init: bfloat16 [2, 1024, 2048], P(None, 'seq', 'mp'), may hold values from -3 to 3
- c_init: float32 [2, 1024, 2048], P(None, 'seq', 'mp'), may hold values from -5 to 5
- embed: bfloat16 [2, 275, 100], replicated, may hold values from -5 to 5
- w_in: bfloat16 [2, 100, 8192], P(None, None, 'mp'), may hold values from -0.625 to 0.625
- w_rec: bfloat16 [2, 2048, 8192], P(None, None, 'mp'), may hold values from -0.125 to 0.125
- bias: float32 [2, 8192], P(None, 'mp'), may hold values from -3 to 3
- w_dec: bfloat16 [2, 2048, 275], P(None, 'mp'), may hold values from -0.75 to 0.75
- b_dec: float32 [2, 275], replicated, may hold values from -3 to 3
Outputs:
- loss: float32 [], replicated
- h_init_grad: float32 [2, 1024, 2048], P(None, 'seq', 'mp')
- c_init_grad: float32 [2, 1024, 2048], P(None, 'seq', 'mp')
- embed_grad: float32 [2, 275, 100], replicated
- w_in_grad: float32 [2, 100, 8192], P(None, None, ('mp', 'seq'))
- w_rec_grad: float32 [2, 2048, 8192], P(None, 'seq', 'mp')
- bias_grad: float32 [2, 8192], P(None, ('mp', 'seq'))
- w_dec_grad: float32 [2, 2048, 275], P(None, ('mp', 'seq'))
- b_dec_grad: float32 [2, 275], replicated
- rms_embed: float32 [2], replicated
- rms_hidden: float32 [2], replicated
- rms_logits: float32 [2], replicated
Inputs may be any that keep to these rules, and one draw needn't show every extreme that they name: `lengths`: they add up to 12288, and the longest stream is valid over all 16 positions. `order`: every stream stands in exactly one slot.
All inputs are finite; a program needn't handle non-finite values.
Results may differ from a plain program's by a relative error of at most 0.018.
Values may be sent and summed in bfloat16 or wider, within the bound.
A program may use at most 256 MiB of HBM per device.

v0:
```python
import jax
import jax.numpy as jnp
from jax import lax
from jax.sharding import PartitionSpec as P


def column_order(own_units):
    lanes = min(128, own_units)
    source = jnp.arange(4 * lanes, dtype=jnp.int32)
    place = source % 4 * lanes + source // 4
    matrix = (place[:, None] == jnp.arange(4 * lanes, dtype=jnp.int32)[None, :]).astype(
        jnp.bfloat16
    )
    return (lanes, matrix)


def grouped(x, matrix):
    width = matrix.shape[0]
    parts = x.reshape(x.shape[:-1] + (x.shape[-1] // width, width))
    out = jnp.einsum("...gc,cp->...gp", parts, matrix, preferred_element_type=jnp.float32)
    return out.astype(x.dtype).reshape(x.shape)


def ungrouped(x, matrix):
    return grouped(x, matrix.T)


def ungrouped_wide(x, lanes):
    parts = x.reshape(x.shape[:-1] + (x.shape[-1] // (4 * lanes), 4, lanes))
    return jnp.swapaxes(parts, -1, -2).reshape(x.shape)


def gates_of(pre, lanes):
    parts = pre.reshape(pre.shape[:-1] + (pre.shape[-1] // (4 * lanes), 4, lanes))
    flat = pre.shape[:-1] + (pre.shape[-1] // 4,)
    return tuple((parts[..., k, :].reshape(flat) for k in range(4)))


def joined_gates(gates, lanes):
    split = [g.reshape(g.shape[:-1] + (g.shape[-1] // lanes, 1, lanes)) for g in gates]
    joined = jnp.concatenate(split, axis=-2)
    return joined.reshape(gates[0].shape[:-1] + (4 * gates[0].shape[-1],))


def recurrences(
    step_ids, own_len, h_init, c_init, embed, w_in, w_rec, bias, w_dec, wd_full, b_dec, count, lanes
):
    length, per_dev = step_ids.shape[1:]
    letter_count = embed.shape[1]
    steps = jnp.arange(length, dtype=jnp.int32)
    live_steps = jnp.stack(
        [steps[:, None] < own_len[None, :], (length - 1 - steps)[:, None] < own_len[None, :]],
        axis=1,
    )[..., None]
    letters = jnp.arange(letter_count, dtype=jnp.int32)
    onehot = (jnp.swapaxes(step_ids, 0, 1)[..., None] == letters).astype(jnp.bfloat16)
    letter_rows = jnp.einsum(
        "sdbv,dve->sdbe", onehot, embed, preferred_element_type=jnp.float32
    ).astype(jnp.bfloat16)
    gates_in = jnp.einsum(
        "sdbe,dec->sdbc", letter_rows, w_in, preferred_element_type=jnp.float32
    ).astype(jnp.bfloat16)

    def forward_step(carry, inputs):
        hidden, cell = carry
        gate_in, live = inputs
        whole = lax.all_gather(hidden, "mp", axis=2, tiled=True)
        recurrent = jnp.einsum("dbh,dhc->dbc", whole, w_rec, preferred_element_type=jnp.float32)
        pre = gate_in.astype(jnp.float32) + recurrent + bias[:, None]
        in_pre, forget_pre, cell_pre, out_pre = gates_of(pre, lanes)
        in_gate, forget, out_gate = (jax.nn.sigmoid(x) for x in (in_pre, forget_pre, out_pre))
        cell_gate = jnp.tanh(cell_pre)
        new_cell = forget * cell + in_gate * cell_gate
        cell_next = jnp.where(live, new_cell, cell)
        hidden_next = jnp.where(
            live, out_gate * jnp.tanh(new_cell), hidden.astype(jnp.float32)
        ).astype(jnp.bfloat16)
        return ((hidden_next, cell_next), (whole, cell, in_gate, forget, cell_gate, out_gate))

    (last_hidden, last_cell), (wholes, cells, *gates) = lax.scan(
        forward_step, (h_init, c_init), (gates_in, live_steps)
    )
    last_whole = lax.all_gather(last_hidden, "mp", axis=2, tiled=True)
    after = jnp.concatenate([wholes[1:], last_whole[None]], axis=0)
    own = h_init.shape[2]
    mine = lax.dynamic_slice_in_dim(after, lax.axis_index("mp") * own, own, axis=3)
    mine_wide = mine.astype(jnp.float32)
    hidden_sq = jnp.sum(jnp.where(live_steps, mine_wide * mine_wide, 0.0), axis=(0, 2, 3))
    logits = (
        jnp.einsum("sdbh,dhv->sdbv", after, wd_full, preferred_element_type=jnp.float32)
        + b_dec[None, :, None]
    )
    targets = jnp.swapaxes(jnp.concatenate([step_ids[:, 1:], step_ids[:, :1]], axis=1), 0, 1)
    fore_valid = steps[:, None] + 1 < own_len[None, :]
    back_valid = (steps[:, None] < length - 1) & ((length - 1 - steps)[:, None] < own_len[None, :])
    valid = jnp.stack([fore_valid, back_valid], axis=1).astype(jnp.float32)
    logit_sq = jnp.sum(valid[..., None] * logits * logits, axis=(0, 2, 3))
    top = jnp.max(logits, axis=-1, keepdims=True)
    log_total = top + jnp.log(jnp.sum(jnp.exp(logits - top), axis=-1, keepdims=True))
    target_hot = targets[..., None] == letters
    picked = jnp.sum(jnp.where(target_hot, logits, 0.0), axis=-1)
    loss = jnp.sum(valid * (log_total[..., 0] - picked))
    grad_logits = (
        valid[..., None] * (jnp.exp(logits - log_total) - target_hot.astype(jnp.float32)) / count
    ).astype(jnp.bfloat16)
    dec_bias = jnp.sum(grad_logits.astype(jnp.float32), axis=(0, 2))
    dec_grad = jnp.einsum("sdbh,sdbv->dhv", mine, grad_logits, preferred_element_type=jnp.float32)

    def backward_step(carry, inputs):
        grad_hidden, grad_cell = carry
        live, cell, in_gate, forget, cell_gate, out_gate, grad_logit = inputs
        grad_hidden = grad_hidden + jnp.einsum(
            "dbv,dhv->dbh", grad_logit, w_dec, preferred_element_type=jnp.float32
        )
        squash = jnp.tanh(forget * cell + in_gate * cell_gate)
        grad_new = jnp.where(
            live, grad_cell + grad_hidden * out_gate * (1.0 - squash * squash), 0.0
        )
        grad_out = jnp.where(live, grad_hidden * squash, 0.0)
        grad_pre = joined_gates(
            [
                grad_new * cell_gate * in_gate * (1.0 - in_gate),
                grad_new * cell * forget * (1.0 - forget),
                grad_new * in_gate * (1.0 - cell_gate * cell_gate),
                grad_out * out_gate * (1.0 - out_gate),
            ],
            lanes,
        ).astype(jnp.bfloat16)
        grad_cell_prev = grad_new * forget + jnp.where(live, 0.0, grad_cell)
        held = jnp.where(live, 0.0, grad_hidden)
        terms = jnp.einsum("dbc,dhc->dbh", grad_pre, w_rec, preferred_element_type=jnp.float32)
        through = lax.psum_scatter(
            terms.astype(jnp.bfloat16), "mp", scatter_dimension=2, tiled=True
        ).astype(jnp.float32)
        return ((held + through, grad_cell_prev), grad_pre)

    start = jnp.zeros(c_init.shape, jnp.float32)
    (hidden_grad, cell_grad), grad_pres = lax.scan(
        backward_step, (start, start), (live_steps, cells, *gates, grad_logits), reverse=True
    )
    rec_grad = jnp.einsum("sdbh,sdbc->dhc", wholes, grad_pres, preferred_element_type=jnp.float32)
    letter_grad = jnp.einsum(
        "sdbv,sdbc->dvc", onehot, grad_pres, preferred_element_type=jnp.float32
    )
    return (
        loss,
        hidden_sq,
        logit_sq,
        dec_bias,
        dec_grad,
        hidden_grad,
        cell_grad,
        rec_grad,
        letter_grad,
    )


def per_device(ids, lengths, order, h_init, c_init, embed, w_in, w_rec, bias, w_dec, b_dec):
    seq_rank = lax.axis_index("seq")
    first_mp = (lax.axis_index("mp") == 0).astype(jnp.float32)
    streams = ids.shape[1]
    per_dev = h_init.shape[1]
    own_units, all_units = (h_init.shape[2], w_rec.shape[1])
    letter_count = embed.shape[1]
    wd_full = lax.all_gather(w_dec, "mp", axis=1, tiled=True)
    whole_ids = lax.all_gather(ids, "seq", axis=0, tiled=True)
    own_order = lax.dynamic_slice_in_dim(order, seq_rank * per_dev, per_dev)
    slot_ids = jnp.take(whole_ids, own_order, axis=1)
    own_len = jnp.take(lengths, own_order)
    live_total = jnp.sum(lengths).astype(jnp.float32)
    count = 2.0 * (jnp.sum(lengths) - streams).astype(jnp.float32)
    step_ids = jnp.stack([slot_ids, jnp.flip(slot_ids, 0)])
    lanes, matrix = column_order(own_units)
    w_rec_grouped = grouped(w_rec, matrix)
    w_in_grouped = grouped(w_in, matrix)
    bias_grouped = jnp.swapaxes(bias.reshape(2, own_units // lanes, lanes, 4), -1, -2).reshape(
        bias.shape
    )
    loss, hidden_sq, logit_sq, dec_bias, dec_grad, hidden_grad, cell_grad, rec_grad, letter_grad = (
        recurrences(
            step_ids,
            own_len,
            h_init,
            c_init,
            embed,
            w_in_grouped,
            w_rec_grouped,
            bias_grouped,
            w_dec,
            wd_full,
            b_dec,
            count,
            lanes,
        )
    )
    embed_wide = embed.astype(jnp.float32)
    in_grad = jnp.einsum("dve,dvc->dec", embed_wide, letter_grad, precision=lax.Precision.HIGHEST)
    bias_grad = jnp.sum(letter_grad, axis=1, keepdims=True)
    embed_part = jnp.einsum(
        "dvc,dec->dve",
        letter_grad,
        w_in_grouped.astype(jnp.float32),
        precision=lax.Precision.HIGHEST,
    )
    edge = ungrouped_wide(jnp.concatenate([in_grad, bias_grad], axis=1), lanes)
    rec_part = lax.psum_scatter(
        rec_grad.astype(jnp.bfloat16), "seq", scatter_dimension=1, tiled=True
    )
    edge_part = lax.psum_scatter(edge.astype(jnp.bfloat16), "seq", scatter_dimension=2, tiled=True)
    dec_part = lax.psum_scatter(
        dec_grad.astype(jnp.bfloat16), "seq", scatter_dimension=1, tiled=True
    )
    loss_sum, hidden_all, logit_all, dec_bias_grad, embed_grad = lax.psum(
        (loss * first_mp, hidden_sq, logit_sq * first_mp, dec_bias * first_mp, embed_part),
        ("seq", "mp"),
    )
    rec_out = ungrouped(rec_part, matrix).astype(jnp.float32)
    rms_embed = jnp.sqrt(jnp.mean(embed_wide * embed_wide, axis=(1, 2)))
    return (
        loss_sum / count,
        hidden_grad,
        cell_grad,
        embed_grad,
        edge_part[:, :-1].astype(jnp.float32),
        rec_out,
        edge_part[:, -1].astype(jnp.float32),
        dec_part.astype(jnp.float32),
        dec_bias_grad,
        rms_embed,
        jnp.sqrt(hidden_all / (all_units * live_total)),
        jnp.sqrt(logit_all / (letter_count * count / 2.0)),
    )


def solution(mesh):
    in_specs = (
        P("seq", None),
        P(),
        P(),
        P(None, "seq", "mp"),
        P(None, "seq", "mp"),
        P(),
        P(None, None, "mp"),
        P(None, None, "mp"),
        P(None, "mp"),
        P(None, "mp", None),
        P(),
    )
    out_specs = (
        P(),
        P(None, "seq", "mp"),
        P(None, "seq", "mp"),
        P(),
        P(None, None, ("mp", "seq")),
        P(None, "seq", "mp"),
        P(None, ("mp", "seq")),
        P(None, ("mp", "seq"), None),
        P(),
        P(),
        P(),
        P(),
    )
    return jax.shard_map(
        per_device, mesh=mesh, in_specs=in_specs, out_specs=out_specs, check_vma=False
    )
```

profile of v0, /device:TPU:0, one launch (start us, length us, event | category | flops | bytes accessed | tf_op | source)
XLA Modules:
  0.0 2771.7 jit_solution(1599841801548186822)
XLA Ops:
  11.5 15.1 all-gather
  30.7 10.4 fusion.44
  41.2 11.9 copy.170
  53.5 10.1 convert_bitcast_fusion
  63.6 1312.1 %while.45 = (s32[]{:T(128)}, bf16[2,256,256]{2,1,0:T(8,128)(2,1)S(1)}, f32[2,256,256]{2,1,0:T(8,128)S(1)}, bf16[16,2,256,2048]{3,2,1,0:T(8,128)(2,1)}, f32[16,2,...) while((s32[]{:T(128)}, ...), condition=%wide.wide.region_1.2_spmd, body=%wide.wide.region_0.1_spmd.sunk | while | flops 2151284736 | bytes 70526840 | solution.py:80
  67.3 29.4 %all-gather.9.cloned.1.call-done = bf16[2,256,2048]{2,1,0:T(8,128)(2,1)} async-done(((bf16[2,256,256]{2,1,0:T(8,128)(2,1)}), bf16[2,256,2048]{2,1,0:T(8,128)(2,1)}) %all-gather.9.cloned.1.call-update) | async-done | bytes 2097168 | tf_op jit(solution)/shard_map/while/body/eval_jaxpr/all_gather | solution.py:67
  105.6 10.6 fusion.142
  150.5 28.2 %all-gather.9.cloned.1.call-done = bf16[2,256,2048]{2,1,0:T(8,128)(2,1)} async-done(((bf16[2,256,256]{2,1,0:T(8,128)(2,1)}), bf16[2,256,2048]{2,1,0:T(8,128)(2,1)}) %all-gather.9.cloned.1.call-update) | async-done | bytes 2097168 | tf_op jit(solution)/shard_map/while/body/eval_jaxpr/all_gather | solution.py:67
  187.7 10.6 fusion.142
  232.6 28.2 %all-gather.9.cloned.1.call-done = bf16[2,256,2048]{2,1,0:T(8,128)(2,1)} async-done(((bf16[2,256,256]{2,1,0:T(8,128)(2,1)}), bf16[2,256,2048]{2,1,0:T(8,128)(2,1)}) %all-gather.9.cloned.1.call-update) | async-done | bytes 2097168 | tf_op jit(solution)/shard_map/while/body/eval_jaxpr/all_gather | solution.py:67
  269.7 10.6 fusion.142
  314.6 27.9 %all-gather.9.cloned.1.call-done = bf16[2,256,2048]{2,1,0:T(8,128)(2,1)} async-done(((bf16[2,256,256]{2,1,0:T(8,128)(2,1)}), bf16[2,256,2048]{2,1,0:T(8,128)(2,1)}) %all-gather.9.cloned.1.call-update) | async-done | bytes 2097168 | tf_op jit(solution)/shard_map/while/body/eval_jaxpr/all_gather | solution.py:67
  351.4 10.6 fusion.142
  396.4 27.9 %all-gather.9.cloned.1.call-done = bf16[2,256,2048]{2,1,0:T(8,128)(2,1)} async-done(((bf16[2,256,256]{2,1,0:T(8,128)(2,1)}), bf16[2,256,2048]{2,1,0:T(8,128)(2,1)}) %all-gather.9.cloned.1.call-update) | async-done | bytes 2097168 | tf_op jit(solution)/shard_map/while/body/eval_jaxpr/all_gather | solution.py:67
  433.2 10.6 fusion.142
  478.2 27.9 %all-gather.9.cloned.1.call-done = bf16[2,256,2048]{2,1,0:T(8,128)(2,1)} async-done(((bf16[2,256,256]{2,1,0:T(8,128)(2,1)}), bf16[2,256,2048]{2,1,0:T(8,128)(2,1)}) %all-gather.9.cloned.1.call-update) | async-done | bytes 2097168 | tf_op jit(solution)/shard_map/while/body/eval_jaxpr/all_gather | solution.py:67
  515.0 10.6 fusion.142
  559.9 28.2 %all-gather.9.cloned.1.call-done = bf16[2,256,2048]{2,1,0:T(8,128)(2,1)} async-done(((bf16[2,256,256]{2,1,0:T(8,128)(2,1)}), bf16[2,256,2048]{2,1,0:T(8,128)(2,1)}) %all-gather.9.cloned.1.call-update) | async-done | bytes 2097168 | tf_op jit(solution)/shard_map/while/body/eval_jaxpr/all_gather | solution.py:67
  597.0 10.6 fusion.142
  641.9 28.2 %all-gather.9.cloned.1.call-done = bf16[2,256,2048]{2,1,0:T(8,128)(2,1)} async-done(((bf16[2,256,256]{2,1,0:T(8,128)(2,1)}), bf16[2,256,2048]{2,1,0:T(8,128)(2,1)}) %all-gather.9.cloned.1.call-update) | async-done | bytes 2097168 | tf_op jit(solution)/shard_map/while/body/eval_jaxpr/all_gather | solution.py:67
  679.1 10.6 fusion.142
  723.9 28.2 %all-gather.9.cloned.1.call-done = bf16[2,256,2048]{2,1,0:T(8,128)(2,1)} async-done(((bf16[2,256,256]{2,1,0:T(8,128)(2,1)}), bf16[2,256,2048]{2,1,0:T(8,128)(2,1)}) %all-gather.9.cloned.1.call-update) | async-done | bytes 2097168 | tf_op jit(solution)/shard_map/while/body/eval_jaxpr/all_gather | solution.py:67
  761.0 10.6 fusion.142
  806.0 27.9 %all-gather.9.cloned.1.call-done = bf16[2,256,2048]{2,1,0:T(8,128)(2,1)} async-done(((bf16[2,256,256]{2,1,0:T(8,128)(2,1)}), bf16[2,256,2048]{2,1,0:T(8,128)(2,1)}) %all-gather.9.cloned.1.call-update) | async-done | bytes 2097168 | tf_op jit(solution)/shard_map/while/body/eval_jaxpr/all_gather | solution.py:67
  842.8 10.6 fusion.142
  887.7 28.2 %all-gather.9.cloned.1.call-done = bf16[2,256,2048]{2,1,0:T(8,128)(2,1)} async-done(((bf16[2,256,256]{2,1,0:T(8,128)(2,1)}), bf16[2,256,2048]{2,1,0:T(8,128)(2,1)}) %all-gather.9.cloned.1.call-update) | async-done | bytes 2097168 | tf_op jit(solution)/shard_map/while/body/eval_jaxpr/all_gather | solution.py:67
  924.8 10.6 fusion.142
  969.7 27.9 %all-gather.9.cloned.1.call-done = bf16[2,256,2048]{2,1,0:T(8,128)(2,1)} async-done(((bf16[2,256,256]{2,1,0:T(8,128)(2,1)}), bf16[2,256,2048]{2,1,0:T(8,128)(2,1)}) %all-gather.9.cloned.1.call-update) | async-done | bytes 2097168 | tf_op jit(solution)/shard_map/while/body/eval_jaxpr/all_gather | solution.py:67
  1006.5 10.6 fusion.142
  1051.5 28.2 %all-gather.9.cloned.1.call-done = bf16[2,256,2048]{2,1,0:T(8,128)(2,1)} async-done(((bf16[2,256,256]{2,1,0:T(8,128)(2,1)}), bf16[2,256,2048]{2,1,0:T(8,128)(2,1)}) %all-gather.9.cloned.1.call-update) | async-done | bytes 2097168 | tf_op jit(solution)/shard_map/while/body/eval_jaxpr/all_gather | solution.py:67
  1088.6 10.6 fusion.142
  1133.5 27.9 %all-gather.9.cloned.1.call-done = bf16[2,256,2048]{2,1,0:T(8,128)(2,1)} async-done(((bf16[2,256,256]{2,1,0:T(8,128)(2,1)}), bf16[2,256,2048]{2,1,0:T(8,128)(2,1)}) %all-gather.9.cloned.1.call-update) | async-done | bytes 2097168 | tf_op jit(solution)/shard_map/while/body/eval_jaxpr/all_gather | solution.py:67
  1170.4 10.6 fusion.142
  1215.3 27.9 %all-gather.9.cloned.1.call-done = bf16[2,256,2048]{2,1,0:T(8,128)(2,1)} async-done(((bf16[2,256,256]{2,1,0:T(8,128)(2,1)}), bf16[2,256,2048]{2,1,0:T(8,128)(2,1)}) %all-gather.9.cloned.1.call-update) | async-done | bytes 2097168 | tf_op jit(solution)/shard_map/while/body/eval_jaxpr/all_gather | solution.py:67
  1252.1 10.6 fusion.142
  1297.0 27.9 %all-gather.9.cloned.1.call-done = bf16[2,256,2048]{2,1,0:T(8,128)(2,1)} async-done(((bf16[2,256,256]{2,1,0:T(8,128)(2,1)}), bf16[2,256,2048]{2,1,0:T(8,128)(2,1)}) %all-gather.9.cloned.1.call-update) | async-done | bytes 2097168 | tf_op jit(solution)/shard_map/while/body/eval_jaxpr/all_gather | solution.py:67
  1333.8 10.6 fusion.142
  1380.9 23.3 copy.172
  1404.2 21.0 slice.40
  1437.4 15.4 bitcast_reduce_fusion
  1470.3 954.1 %while.44 = (s32[]{:T(128)}, f32[2,256,256]{1,2,0:T(8,128)}, f32[2,256,256]{1,2,0:T(8,128)}, bf16[16,2,256,1024]{3,2,1,0:T(8,128)(2,1)}, pred[16,2,256,1]{2,1,3,...) while((s32[]{:T(128)}, f32[2,256,256]{1,2,0:T(8,128)}, ...), condition=%wide.region_10.11_spmd.clone, body=%wide.region_8.10_spmd.clone.sunk | while | flops 2227306496 | bytes 52475628 | solution.py:138
  1488.5 39.5 %reduce-scatter.11.cloned.1.call-done = bf16[2,256,256]{1,2,0:T(8,128)(2,1)} async-done(((bf16[2,256,2048]{1,2,0:T(8,128)(2,1)}), bf16[2,256,256]{1,2,0:T(8,128)(2,1)}) %reduce-scatter.11.cloned.1.call-update) | async-done | bytes 262160 | tf_op jit(solution)/shard_map/while/body/eval_jaxpr/reduce_scatter | solution.py:132
  1548.2 39.5 %reduce-scatter.11.cloned.1.call-done = bf16[2,256,256]{1,2,0:T(8,128)(2,1)} async-done(((bf16[2,256,2048]{1,2,0:T(8,128)(2,1)}), bf16[2,256,256]{1,2,0:T(8,128)(2,1)}) %reduce-scatter.11.cloned.1.call-update) | async-done | bytes 262160 | tf_op jit(solution)/shard_map/while/body/eval_jaxpr/reduce_scatter | solution.py:132
  1607.8 39.5 %reduce-scatter.11.cloned.1.call-done = bf16[2,256,256]{1,2,0:T(8,128)(2,1)} async-done(((bf16[2,256,2048]{1,2,0:T(8,128)(2,1)}), bf16[2,256,256]{1,2,0:T(8,128)(2,1)}) %reduce-scatter.11.cloned.1.call-update) | async-done | bytes 262160 | tf_op jit(solution)/shard_map/while/body/eval_jaxpr/reduce_scatter | solution.py:132
  1667.4 39.6 %reduce-scatter.11.cloned.1.call-done = bf16[2,256,256]{1,2,0:T(8,128)(2,1)} async-done(((bf16[2,256,2048]{1,2,0:T(8,128)(2,1)}), bf16[2,256,256]{1,2,0:T(8,128)(2,1)}) %reduce-scatter.11.cloned.1.call-update) | async-done | bytes 262160 | tf_op jit(solution)/shard_map/while/body/eval_jaxpr/reduce_scatter | solution.py:132
  1727.0 39.6 %reduce-scatter.11.cloned.1.call-done = bf16[2,256,256]{1,2,0:T(8,128)(2,1)} async-done(((bf16[2,256,2048]{1,2,0:T(8,128)(2,1)}), bf16[2,256,256]{1,2,0:T(8,128)(2,1)}) %reduce-scatter.11.cloned.1.call-update) | async-done | bytes 262160 | tf_op jit(solution)/shard_map/while/body/eval_jaxpr/reduce_scatter | solution.py:132
  1786.7 39.5 %reduce-scatter.11.cloned.1.call-done = bf16[2,256,256]{1,2,0:T(8,128)(2,1)} async-done(((bf16[2,256,2048]{1,2,0:T(8,128)(2,1)}), bf16[2,256,256]{1,2,0:T(8,128)(2,1)}) %reduce-scatter.11.cloned.1.call-update) | async-done | bytes 262160 | tf_op jit(solution)/shard_map/while/body/eval_jaxpr/reduce_scatter | solution.py:132
  1846.3 39.5 %reduce-scatter.11.cloned.1.call-done = bf16[2,256,256]{1,2,0:T(8,128)(2,1)} async-done(((bf16[2,256,2048]{1,2,0:T(8,128)(2,1)}), bf16[2,256,256]{1,2,0:T(8,128)(2,1)}) %reduce-scatter.11.cloned.1.call-update) | async-done | bytes 262160 | tf_op jit(solution)/shard_map/while/body/eval_jaxpr/reduce_scatter | solution.py:132
  1905.9 39.6 %reduce-scatter.11.cloned.1.call-done = bf16[2,256,256]{1,2,0:T(8,128)(2,1)} async-done(((bf16[2,256,2048]{1,2,0:T(8,128)(2,1)}), bf16[2,256,256]{1,2,0:T(8,128)(2,1)}) %reduce-scatter.11.cloned.1.call-update) | async-done | bytes 262160 | tf_op jit(solution)/shard_map/while/body/eval_jaxpr/reduce_scatter | solution.py:132
  1965.6 39.5 %reduce-scatter.11.cloned.1.call-done = bf16[2,256,256]{1,2,0:T(8,128)(2,1)} async-done(((bf16[2,256,2048]{1,2,0:T(8,128)(2,1)}), bf16[2,256,256]{1,2,0:T(8,128)(2,1)}) %reduce-scatter.11.cloned.1.call-update) | async-done | bytes 262160 | tf_op jit(solution)/shard_map/while/body/eval_jaxpr/reduce_scatter | solution.py:132
  2025.2 39.5 %reduce-scatter.11.cloned.1.call-done = bf16[2,256,256]{1,2,0:T(8,128)(2,1)} async-done(((bf16[2,256,2048]{1,2,0:T(8,128)(2,1)}), bf16[2,256,256]{1,2,0:T(8,128)(2,1)}) %reduce-scatter.11.cloned.1.call-update) | async-done | bytes 262160 | tf_op jit(solution)/shard_map/while/body/eval_jaxpr/reduce_scatter | solution.py:132
  2084.8 39.6 %reduce-scatter.11.cloned.1.call-done = bf16[2,256,256]{1,2,0:T(8,128)(2,1)} async-done(((bf16[2,256,2048]{1,2,0:T(8,128)(2,1)}), bf16[2,256,256]{1,2,0:T(8,128)(2,1)}) %reduce-scatter.11.cloned.1.call-update) | async-done | bytes 262160 | tf_op jit(solution)/shard_map/while/body/eval_jaxpr/reduce_scatter | solution.py:132
  2144.4 39.6 %reduce-scatter.11.cloned.1.call-done = bf16[2,256,256]{1,2,0:T(8,128)(2,1)} async-done(((bf16[2,256,2048]{1,2,0:T(8,128)(2,1)}), bf16[2,256,256]{1,2,0:T(8,128)(2,1)}) %reduce-scatter.11.cloned.1.call-update) | async-done | bytes 262160 | tf_op jit(solution)/shard_map/while/body/eval_jaxpr/reduce_scatter | solution.py:132
  2204.2 39.5 %reduce-scatter.11.cloned.1.call-done = bf16[2,256,256]{1,2,0:T(8,128)(2,1)} async-done(((bf16[2,256,2048]{1,2,0:T(8,128)(2,1)}), bf16[2,256,256]{1,2,0:T(8,128)(2,1)}) %reduce-scatter.11.cloned.1.call-update) | async-done | bytes 262160 | tf_op jit(solution)/shard_map/while/body/eval_jaxpr/reduce_scatter | solution.py:132
  2263.7 39.6 %reduce-scatter.11.cloned.1.call-done = bf16[2,256,256]{1,2,0:T(8,128)(2,1)} async-done(((bf16[2,256,2048]{1,2,0:T(8,128)(2,1)}), bf16[2,256,256]{1,2,0:T(8,128)(2,1)}) %reduce-scatter.11.cloned.1.call-update) | async-done | bytes 262160 | tf_op jit(solution)/shard_map/while/body/eval_jaxpr/reduce_scatter | solution.py:132
  2323.4 39.5 %reduce-scatter.11.cloned.1.call-done = bf16[2,256,256]{1,2,0:T(8,128)(2,1)} async-done(((bf16[2,256,2048]{1,2,0:T(8,128)(2,1)}), bf16[2,256,256]{1,2,0:T(8,128)(2,1)}) %reduce-scatter.11.cloned.1.call-update) | async-done | bytes 262160 | tf_op jit(solution)/shard_map/while/body/eval_jaxpr/reduce_scatter | solution.py:132
  2383.0 39.6 %reduce-scatter.11.cloned.1.call-done = bf16[2,256,256]{1,2,0:T(8,128)(2,1)} async-done(((bf16[2,256,2048]{1,2,0:T(8,128)(2,1)}), bf16[2,256,256]{1,2,0:T(8,128)(2,1)}) %reduce-scatter.11.cloned.1.call-update) | async-done | bytes 262160 | tf_op jit(solution)/shard_map/while/body/eval_jaxpr/reduce_scatter | solution.py:132
  2424.4 8.6 bitcast_reduce_fusion.1
  2445.5 42.9 %bitcast_convert_fusion = bf16[2,2048,1024]{2,1,0:T(8,128)(2,1)} fusion(bf16[16,2,256,2048]{3,2,1,0:T(8,128)(2,1)} %get-tuple-element.342, bf16[16,2,256,1024]{3,2,1,0:T(8,128)(2,1)} %get-tuple-element.351), kind=kOutput, calls=%fused_computation.74 | convolution fusion | flops 34363932672 | bytes 58720256 | tf_op jit(solution)/shard_map/sdbh,sdbc->dhc/dot_general | solution.py:141
  2490.9 39.7 %all-reduce = (f32[]{:T(128)}, f32[2,275]{1,0:T(2,128)}, f32[2]{0:T(128)S(1)}, f32[2]{0:T(128)S(1)}) all-reduce(f32[]{:T(128)S(6)} %mul.239, f32[2,275]{1,0:T(2,128)S(1)} %broadcast_multiply_fusion, f32[2]{0:T(128)S(1)} %copy-done.23, f32[2]{0:T(128)S(1)} %broadcast_multiply_fusion.1), channel_id=1, replica_groups=mesh['seq'=4,'mp'=8] {'seq','mp'}, use_global_device_ids=true, to_apply=%region_6.7 | all-reduce | flops 555 | bytes 4440 | tf_op jit(solution)/shard_map/psum | solution.py:213
  2534.3 26.0 all-reduce.3.cloned.1.call-done
  2562.1 22.2 reduce-scatter.9.cloned.1.call-done
  2585.9 20.9 reduce-scatter.5.cloned.1.call-done
  2610.2 141.8 %reduce-scatter.7.cloned.1.call-done = bf16[2,512,1024]{2,1,0:T(8,128)(2,1)} async-done(((bf16[2,2048,1024]{2,1,0:T(8,128)(2,1)}), bf16[2,512,1024]{2,1,0:T(8,128)(2,1)}) %reduce-scatter.7.cloned.1.call-update) | async-done | bytes 2097168 | tf_op jit(solution)/shard_map/reduce_scatter | solution.py:206
  (959 shorter events, 1085.6 us)
Async XLA Ops:
  63.6 1314.6 %copy-start.1 = (s32[1024]{0:T(1024)S(1)}, s32[1024]{0:T(1024)}, u32[]{:S(2)}) copy-start(s32[1024]{0:T(1024)} %param.16) | copy-start | bytes 12292
  63.9 32.8 %all-gather.9.cloned.1.call-start = ((), (), s32[]{:S(2)}) async-start(), calls=%async_computation.11 | async-start | bytes 2359296 | tf_op jit(solution)/shard_map/while/body/eval_jaxpr/all_gather | solution.py:67
  105.6 38.3 %copy-start.3 = (f32[2,256,256]{2,1,0:T(8,128)S(1)}, f32[2,256,256]{2,1,0:T(8,128)}, u32[]{:S(2)}) copy-start(f32[2,256,256]{2,1,0:T(8,128)} %copy-done.2) | copy-start | bytes 1572868 | tf_op jit(solution)/shard_map/while
  105.6 38.3 %copy-start.6 = (bf16[2,256,256]{2,1,0:T(8,128)(2,1)S(1)}, bf16[2,256,256]{2,1,0:T(8,128)(2,1)}, u32[]{:S(2)}) copy-start(bf16[2,256,256]{2,1,0:T(8,128)(2,1)} %copy-done.5) | copy-start | bytes 786436 | tf_op jit(solution)/shard_map/while
  147.1 31.7 %all-gather.9.cloned.1.call-start = ((), (), s32[]{:S(2)}) async-start(), calls=%async_computation.11 | async-start | bytes 2359296 | tf_op jit(solution)/shard_map/while/body/eval_jaxpr/all_gather | solution.py:67
  229.1 31.7 %all-gather.9.cloned.1.call-start = ((), (), s32[]{:S(2)}) async-start(), calls=%async_computation.11 | async-start | bytes 2359296 | tf_op jit(solution)/shard_map/while/body/eval_jaxpr/all_gather | solution.py:67
  311.1 31.3 %all-gather.9.cloned.1.call-start = ((), (), s32[]{:S(2)}) async-start(), calls=%async_computation.11 | async-start | bytes 2359296 | tf_op jit(solution)/shard_map/while/body/eval_jaxpr/all_gather | solution.py:67
  351.4 38.3 %copy-start.3 = (f32[2,256,256]{2,1,0:T(8,128)S(1)}, f32[2,256,256]{2,1,0:T(8,128)}, u32[]{:S(2)}) copy-start(f32[2,256,256]{2,1,0:T(8,128)} %copy-done.2) | copy-start | bytes 1572868 | tf_op jit(solution)/shard_map/while
  351.4 38.3 %copy-start.6 = (bf16[2,256,256]{2,1,0:T(8,128)(2,1)S(1)}, bf16[2,256,256]{2,1,0:T(8,128)(2,1)}, u32[]{:S(2)}) copy-start(bf16[2,256,256]{2,1,0:T(8,128)(2,1)} %copy-done.5) | copy-start | bytes 786436 | tf_op jit(solution)/shard_map/while
  392.9 31.4 %all-gather.9.cloned.1.call-start = ((), (), s32[]{:S(2)}) async-start(), calls=%async_computation.11 | async-start | bytes 2359296 | tf_op jit(solution)/shard_map/while/body/eval_jaxpr/all_gather | solution.py:67
  433.2 38.3 %copy-start.3 = (f32[2,256,256]{2,1,0:T(8,128)S(1)}, f32[2,256,256]{2,1,0:T(8,128)}, u32[]{:S(2)}) copy-start(f32[2,256,256]{2,1,0:T(8,128)} %copy-done.2) | copy-start | bytes 1572868 | tf_op jit(solution)/shard_map/while
  433.2 38.3 %copy-start.6 = (bf16[2,256,256]{2,1,0:T(8,128)(2,1)S(1)}, bf16[2,256,256]{2,1,0:T(8,128)(2,1)}, u32[]{:S(2)}) copy-start(bf16[2,256,256]{2,1,0:T(8,128)(2,1)} %copy-done.5) | copy-start | bytes 786436 | tf_op jit(solution)/shard_map/while
  474.7 31.3 %all-gather.9.cloned.1.call-start = ((), (), s32[]{:S(2)}) async-start(), calls=%async_computation.11 | async-start | bytes 2359296 | tf_op jit(solution)/shard_map/while/body/eval_jaxpr/all_gather | solution.py:67
  515.0 38.3 %copy-start.3 = (f32[2,256,256]{2,1,0:T(8,128)S(1)}, f32[2,256,256]{2,1,0:T(8,128)}, u32[]{:S(2)}) copy-start(f32[2,256,256]{2,1,0:T(8,128)} %copy-done.2) | copy-start | bytes 1572868 | tf_op jit(solution)/shard_map/while
  515.0 38.3 %copy-start.6 = (bf16[2,256,256]{2,1,0:T(8,128)(2,1)S(1)}, bf16[2,256,256]{2,1,0:T(8,128)(2,1)}, u32[]{:S(2)}) copy-start(bf16[2,256,256]{2,1,0:T(8,128)(2,1)} %copy-done.5) | copy-start | bytes 786436 | tf_op jit(solution)/shard_map/while
  556.5 31.7 %all-gather.9.cloned.1.call-start = ((), (), s32[]{:S(2)}) async-start(), calls=%async_computation.11 | async-start | bytes 2359296 | tf_op jit(solution)/shard_map/while/body/eval_jaxpr/all_gather | solution.py:67
  638.5 31.7 %all-gather.9.cloned.1.call-start = ((), (), s32[]{:S(2)}) async-start(), calls=%async_computation.11 | async-start | bytes 2359296 | tf_op jit(solution)/shard_map/while/body/eval_jaxpr/all_gather | solution.py:67
  720.5 31.7 %all-gather.9.cloned.1.call-start = ((), (), s32[]{:S(2)}) async-start(), calls=%async_computation.11 | async-start | bytes 2359296 | tf_op jit(solution)/shard_map/while/body/eval_jaxpr/all_gather | solution.py:67
  761.0 38.3 %copy-start.3 = (f32[2,256,256]{2,1,0:T(8,128)S(1)}, f32[2,256,256]{2,1,0:T(8,128)}, u32[]{:S(2)}) copy-start(f32[2,256,256]{2,1,0:T(8,128)} %copy-done.2) | copy-start | bytes 1572868 | tf_op jit(solution)/shard_map/while
  761.0 38.3 %copy-start.6 = (bf16[2,256,256]{2,1,0:T(8,128)(2,1)S(1)}, bf16[2,256,256]{2,1,0:T(8,128)(2,1)}, u32[]{:S(2)}) copy-start(bf16[2,256,256]{2,1,0:T(8,128)(2,1)} %copy-done.5) | copy-start | bytes 786436 | tf_op jit(solution)/shard_map/while
  802.6 31.4 %all-gather.9.cloned.1.call-start = ((), (), s32[]{:S(2)}) async-start(), calls=%async_computation.11 | async-start | bytes 2359296 | tf_op jit(solution)/shard_map/while/body/eval_jaxpr/all_gather | solution.py:67
  842.8 38.3 %copy-start.3 = (f32[2,256,256]{2,1,0:T(8,128)S(1)}, f32[2,256,256]{2,1,0:T(8,128)}, u32[]{:S(2)}) copy-start(f32[2,256,256]{2,1,0:T(8,128)} %copy-done.2) | copy-start | bytes 1572868 | tf_op jit(solution)/shard_map/while
  842.8 38.3 %copy-start.6 = (bf16[2,256,256]{2,1,0:T(8,128)(2,1)S(1)}, bf16[2,256,256]{2,1,0:T(8,128)(2,1)}, u32[]{:S(2)}) copy-start(bf16[2,256,256]{2,1,0:T(8,128)(2,1)} %copy-done.5) | copy-start | bytes 786436 | tf_op jit(solution)/shard_map/while
  884.3 31.7 %all-gather.9.cloned.1.call-start = ((), (), s32[]{:S(2)}) async-start(), calls=%async_computation.11 | async-start | bytes 2359296 | tf_op jit(solution)/shard_map/while/body/eval_jaxpr/all_gather | solution.py:67
  966.3 31.3 %all-gather.9.cloned.1.call-start = ((), (), s32[]{:S(2)}) async-start(), calls=%async_computation.11 | async-start | bytes 2359296 | tf_op jit(solution)/shard_map/while/body/eval_jaxpr/all_gather | solution.py:67
  1006.5 38.2 %copy-start.6 = (bf16[2,256,256]{2,1,0:T(8,128)(2,1)S(1)}, bf16[2,256,256]{2,1,0:T(8,128)(2,1)}, u32[]{:S(2)}) copy-start(bf16[2,256,256]{2,1,0:T(8,128)(2,1)} %copy-done.5) | copy-start | bytes 786436 | tf_op jit(solution)/shard_map/while
  1048.0 31.7 %all-gather.9.cloned.1.call-start = ((), (), s32[]{:S(2)}) async-start(), calls=%async_computation.11 | async-start | bytes 2359296 | tf_op jit(solution)/shard_map/while/body/eval_jaxpr/all_gather | solution.py:67
  1088.6 38.3 %copy-start.3 = (f32[2,256,256]{2,1,0:T(8,128)S(1)}, f32[2,256,256]{2,1,0:T(8,128)}, u32[]{:S(2)}) copy-start(f32[2,256,256]{2,1,0:T(8,128)} %copy-done.2) | copy-start | bytes 1572868 | tf_op jit(solution)/shard_map/while
  1088.6 38.3 %copy-start.6 = (bf16[2,256,256]{2,1,0:T(8,128)(2,1)S(1)}, bf16[2,256,256]{2,1,0:T(8,128)(2,1)}, u32[]{:S(2)}) copy-start(bf16[2,256,256]{2,1,0:T(8,128)(2,1)} %copy-done.5) | copy-start | bytes 786436 | tf_op jit(solution)/shard_map/while
  1130.1 31.3 %all-gather.9.cloned.1.call-start = ((), (), s32[]{:S(2)}) async-start(), calls=%async_computation.11 | async-start | bytes 2359296 | tf_op jit(solution)/shard_map/while/body/eval_jaxpr/all_gather | solution.py:67
  1170.4 38.3 %copy-start.3 = (f32[2,256,256]{2,1,0:T(8,128)S(1)}, f32[2,256,256]{2,1,0:T(8,128)}, u32[]{:S(2)}) copy-start(f32[2,256,256]{2,1,0:T(8,128)} %copy-done.2) | copy-start | bytes 1572868 | tf_op jit(solution)/shard_map/while
  1170.4 38.3 %copy-start.6 = (bf16[2,256,256]{2,1,0:T(8,128)(2,1)S(1)}, bf16[2,256,256]{2,1,0:T(8,128)(2,1)}, u32[]{:S(2)}) copy-start(bf16[2,256,256]{2,1,0:T(8,128)(2,1)} %copy-done.5) | copy-start | bytes 786436 | tf_op jit(solution)/shard_map/while
  1211.9 31.4 %all-gather.9.cloned.1.call-start = ((), (), s32[]{:S(2)}) async-start(), calls=%async_computation.11 | async-start | bytes 2359296 | tf_op jit(solution)/shard_map/while/body/eval_jaxpr/all_gather | solution.py:67
  1252.1 38.2 %copy-start.3 = (f32[2,256,256]{2,1,0:T(8,128)S(1)}, f32[2,256,256]{2,1,0:T(8,128)}, u32[]{:S(2)}) copy-start(f32[2,256,256]{2,1,0:T(8,128)} %copy-done.2) | copy-start | bytes 1572868 | tf_op jit(solution)/shard_map/while
  1252.1 38.2 %copy-start.6 = (bf16[2,256,256]{2,1,0:T(8,128)(2,1)S(1)}, bf16[2,256,256]{2,1,0:T(8,128)(2,1)}, u32[]{:S(2)}) copy-start(bf16[2,256,256]{2,1,0:T(8,128)(2,1)} %copy-done.5) | copy-start | bytes 786436 | tf_op jit(solution)/shard_map/while
  1293.6 31.3 %all-gather.9.cloned.1.call-start = ((), (), s32[]{:S(2)}) async-start(), calls=%async_computation.11 | async-start | bytes 2359296 | tf_op jit(solution)/shard_map/while/body/eval_jaxpr/all_gather | solution.py:67
  1333.8 38.2 %copy-start.3 = (f32[2,256,256]{2,1,0:T(8,128)S(1)}, f32[2,256,256]{2,1,0:T(8,128)}, u32[]{:S(2)}) copy-start(f32[2,256,256]{2,1,0:T(8,128)} %copy-done.2) | copy-start | bytes 1572868 | tf_op jit(solution)/shard_map/while
  1333.8 38.2 %copy-start.6 = (bf16[2,256,256]{2,1,0:T(8,128)(2,1)S(1)}, bf16[2,256,256]{2,1,0:T(8,128)(2,1)}, u32[]{:S(2)}) copy-start(bf16[2,256,256]{2,1,0:T(8,128)(2,1)} %copy-done.5) | copy-start | bytes 786436 | tf_op jit(solution)/shard_map/while
  1375.7 50.2 %all-gather.5.cloned.1.call-start = ((), (), s32[]{:S(2)}) async-start(), calls=%async_computation.4 | async-start | bytes 2359296 | tf_op jit(solution)/shard_map/all_gather | solution.py:83
  1376.4 60.9 %all-gather.7.cloned.1.call-start = ((), (), s32[]{:S(2)}) async-start(), calls=%async_computation.5 | async-start | bytes 2580480 | tf_op jit(solution)/shard_map/all_gather | solution.py:165
  1470.3 954.1 %copy-start.18 = (s32[16,2,256]{2,0,1:T(8,128)S(1)}, s32[16,2,256]{2,0,1:T(8,128)}, u32[]{:S(2)}) copy-start(s32[16,2,256]{2,0,1:T(8,128)} %copy-done.17) | copy-start | bytes 98308
  1470.5 57.6 %reduce-scatter.11.cloned.1.call-start = ((), (), s32[]{:S(2)}) async-start(), calls=%async_computation.10 | async-start | bytes 2359296 | tf_op jit(solution)/shard_map/while/body/eval_jaxpr/reduce_scatter | solution.py:132
  1529.8 57.8 %reduce-scatter.11.cloned.1.call-start = ((), (), s32[]{:S(2)}) async-start(), calls=%async_computation.10 | async-start | bytes 2359296 | tf_op jit(solution)/shard_map/while/body/eval_jaxpr/reduce_scatter | solution.py:132
  1589.5 57.8 %reduce-scatter.11.cloned.1.call-start = ((), (), s32[]{:S(2)}) async-start(), calls=%async_computation.10 | async-start | bytes 2359296 | tf_op jit(solution)/shard_map/while/body/eval_jaxpr/reduce_scatter | solution.py:132
  1649.1 57.8 %reduce-scatter.11.cloned.1.call-start = ((), (), s32[]{:S(2)}) async-start(), calls=%async_computation.10 | async-start | bytes 2359296 | tf_op jit(solution)/shard_map/while/body/eval_jaxpr/reduce_scatter | solution.py:132
  1708.7 57.8 %reduce-scatter.11.cloned.1.call-start = ((), (), s32[]{:S(2)}) async-start(), calls=%async_computation.10 | async-start | bytes 2359296 | tf_op jit(solution)/shard_map/while/body/eval_jaxpr/reduce_scatter | solution.py:132
  1768.4 57.8 %reduce-scatter.11.cloned.1.call-start = ((), (), s32[]{:S(2)}) async-start(), calls=%async_computation.10 | async-start | bytes 2359296 | tf_op jit(solution)/shard_map/while/body/eval_jaxpr/reduce_scatter | solution.py:132
  1828.0 57.8 %reduce-scatter.11.cloned.1.call-start = ((), (), s32[]{:S(2)}) async-start(), calls=%async_computation.10 | async-start | bytes 2359296 | tf_op jit(solution)/shard_map/while/body/eval_jaxpr/reduce_scatter | solution.py:132
  1887.6 57.8 %reduce-scatter.11.cloned.1.call-start = ((), (), s32[]{:S(2)}) async-start(), calls=%async_computation.10 | async-start | bytes 2359296 | tf_op jit(solution)/shard_map/while/body/eval_jaxpr/reduce_scatter | solution.py:132
  1947.3 57.8 %reduce-scatter.11.cloned.1.call-start = ((), (), s32[]{:S(2)}) async-start(), calls=%async_computation.10 | async-start | bytes 2359296 | tf_op jit(solution)/shard_map/while/body/eval_jaxpr/reduce_scatter | solution.py:132
  2006.9 57.8 %reduce-scatter.11.cloned.1.call-start = ((), (), s32[]{:S(2)}) async-start(), calls=%async_computation.10 | async-start | bytes 2359296 | tf_op jit(solution)/shard_map/while/body/eval_jaxpr/reduce_scatter | solution.py:132
  2066.5 57.8 %reduce-scatter.11.cloned.1.call-start = ((), (), s32[]{:S(2)}) async-start(), calls=%async_computation.10 | async-start | bytes 2359296 | tf_op jit(solution)/shard_map/while/body/eval_jaxpr/reduce_scatter | solution.py:132
  2126.2 57.9 %reduce-scatter.11.cloned.1.call-start = ((), (), s32[]{:S(2)}) async-start(), calls=%async_computation.10 | async-start | bytes 2359296 | tf_op jit(solution)/shard_map/while/body/eval_jaxpr/reduce_scatter | solution.py:132
  2185.8 57.8 %reduce-scatter.11.cloned.1.call-start = ((), (), s32[]{:S(2)}) async-start(), calls=%async_computation.10 | async-start | bytes 2359296 | tf_op jit(solution)/shard_map/while/body/eval_jaxpr/reduce_scatter | solution.py:132
  2245.4 57.9 %reduce-scatter.11.cloned.1.call-start = ((), (), s32[]{:S(2)}) async-start(), calls=%async_computation.10 | async-start | bytes 2359296 | tf_op jit(solution)/shard_map/while/body/eval_jaxpr/reduce_scatter | solution.py:132
  2305.1 57.8 %reduce-scatter.11.cloned.1.call-start = ((), (), s32[]{:S(2)}) async-start(), calls=%async_computation.10 | async-start | bytes 2359296 | tf_op jit(solution)/shard_map/while/body/eval_jaxpr/reduce_scatter | solution.py:132
  2364.7 57.9 %reduce-scatter.11.cloned.1.call-start = ((), (), s32[]{:S(2)}) async-start(), calls=%async_computation.10 | async-start | bytes 2359296 | tf_op jit(solution)/shard_map/while/body/eval_jaxpr/reduce_scatter | solution.py:132
  2424.4 135.9 %all-reduce.3.cloned.1.call-start = ((), (), s32[]{:S(2)}) async-start(), calls=%async_computation.6 | async-start | bytes 573440 | tf_op jit(solution)/shard_map/psum | solution.py:213
  2434.9 149.4 %reduce-scatter.9.cloned.1.call-start = ((), (), s32[]{:S(2)}) async-start(), calls=%async_computation.9 | async-start | bytes 491520 | tf_op jit(solution)/shard_map/reduce_scatter | solution.py:210
  2442.2 164.5 %reduce-scatter.5.cloned.1.call-start = ((), (), s32[]{:S(2)}) async-start(), calls=%async_computation.7 | async-start | bytes 655360 | tf_op jit(solution)/shard_map/reduce_scatter | solution.py:209
  2445.3 306.8 %reduce-scatter.7.cloned.1.call-start = ((), (), s32[]{:S(2)}) async-start(), calls=%async_computation.8 | async-start | bytes 10485760 | tf_op jit(solution)/shard_map/reduce_scatter | solution.py:206
  2488.5 42.2 %copy-start.9 = (f32[2,256,256]{1,2,0:T(8,128)S(1)}, f32[2,256,256]{1,2,0:T(8,128)}, u32[]{:S(2)}) copy-start(f32[2,256,256]{1,2,0:T(8,128)} %get-tuple-element.535) | copy-start | bytes 1572868
  2488.5 43.1 %copy-start.10 = (f32[2,256,256]{1,2,0:T(8,128)S(1)}, f32[2,256,256]{1,2,0:T(8,128)}, u32[]{:S(2)}) copy-start(f32[2,256,256]{1,2,0:T(8,128)} %get-tuple-element.536) | copy-start | bytes 1572868
  2488.5 263.6 %copy-start.25 = (s32[512]{0:T(512)S(1)}, s32[512]{0:T(512)}, u32[]{:S(2)}) copy-start(s32[512]{0:T(512)} %copy-done.24) | copy-start | bytes 6148
  (76 other events, 1550.4 us)
Sparse Core Ops, SparseCore 0:
  67.3 29.3 all-gather.8
  150.6 28.1 all-gather.8
  232.6 28.1 all-gather.8
  314.3 28.1 all-gather.8
  396.1 28.1 all-gather.8
  477.9 28.1 all-gather.8
  559.9 28.1 all-gather.8
  641.9 28.1 all-gather.8
  723.9 28.1 all-gather.8
  805.7 28.1 all-gather.8
  887.7 28.1 all-gather.8
  969.4 28.1 all-gather.8
  1051.5 28.1 all-gather.8
  1133.2 28.1 all-gather.8
  1215.0 28.1 all-gather.8
  1296.7 28.1 all-gather.8
  1486.8 41.2 reduce-scatter.10
  1546.4 41.1 reduce-scatter.10
  1606.1 41.1 reduce-scatter.10
  1665.7 41.1 reduce-scatter.10
  1725.3 41.1 reduce-scatter.10
  1784.9 41.1 reduce-scatter.10
  1844.6 41.1 reduce-scatter.10
  1904.2 41.1 reduce-scatter.10
  1963.8 41.2 reduce-scatter.10
  2023.5 41.1 reduce-scatter.10
  2083.1 41.1 reduce-scatter.10
  2142.7 41.2 reduce-scatter.10
  2202.4 41.1 reduce-scatter.10
  2262.0 41.2 reduce-scatter.10
  2321.7 41.1 reduce-scatter.10
  2381.3 41.2 reduce-scatter.10
Sparse Core Ops, SparseCore 1:
  1378.7 28.0 all-gather.4
  1408.4 28.9 all-gather.6
  2435.0 125.2 all-reduce.2
  2562.7 21.5 reduce-scatter.8
  2587.2 19.6 reduce-scatter.4
  2609.2 142.8 reduce-scatter.6
where the time goes:
time: 2790 us; the launch traced here: 2770 us
  waiting for transfers between devices  1300 us (47%)
  local copies, waits for them, and re-layouts  638 us (23%)
  other arithmetic  398 us (14%)
  matrix products  358 us (13%)
  blocking collectives  54.8 us (2%)
    reduce_scatter x16, waiting for transfers between devices, backward_step(): lax.psum_scatter(terms.astype(jnp.bfloat16), 'mp', scatter_dimension=2, t...  633 us
    all_gather x16, waiting for transfers between devices, forward_step(): whole = lax.all_gather(hidden, 'mp', axis=2, tiled=True)  450 us
    div x96, local copies, waits for them, and re-layouts, forward_step(): jax.nn.sigmoid(x)  173 us
    div x16, other arithmetic, forward_step(): jax.nn.sigmoid(x)  170 us
    reduce_scatter x1, waiting for transfers between devices, per_device(): lax.psum_scatter(rec_grad.astype(jnp.bfloat16), 'seq', scatter_dimension=...  142 us
    tanh x16, other arithmetic, forward_step(): cell_gate = jnp.tanh(cell_pre)  133 us
    dot_general x16, matrix products, backward_step(): jnp.einsum('dbc,dhc->dbh', grad_pre, w_rec, preferred_element_type=jnp.fl...  113 us
    dynamic_update_slice x64, local copies, waits for them, and re-layouts, recurrences(): lax.scan(forward_step, (h_init, c_init), (gates_in, live_steps))  110 us
  transfers between devices with their start and end apart: 38, of which 37 were waited for; matrix products, arithmetic and copies ran while one was open for 7% of the time, Pallas kernels for 0%

commit v1 on v0

--- a/solution.py
+++ b/solution.py
@@ -211,8 +211,11 @@
         dec_grad.astype(jnp.bfloat16), "seq", scatter_dimension=1, tiled=True
     )
     loss_sum, hidden_all, logit_all, dec_bias_grad, embed_grad = lax.psum(
-        (loss * first_mp, hidden_sq, logit_sq * first_mp, dec_bias * first_mp, embed_part),
-        ("seq", "mp"),
+        lax.psum(
+            (loss * first_mp, hidden_sq, logit_sq * first_mp, dec_bias * first_mp, embed_part),
+            "seq",
+        ),
+        "mp",
     )
     rec_out = ungrouped(rec_part, matrix).astype(jnp.float32)
     rms_embed = jnp.sqrt(jnp.mean(embed_wide * embed_wide, axis=(1, 2)))

time: 2790 us -> 2750 us (0.986)
    psum x1, blocking collectives: 39.7 us -> 11.1 us  [per_device(): lax.psum((loss * first_mp, hidden_sq, logit_sq * first_mp, dec_bias * fir...]
  transfers between devices with their start and end apart: 38 -> 39, of which waited for: 37 -> 36; matrix products, arithmetic and copies ran while one was open for 7% -> 7% of each run, Pallas kernels for 0% -> 0%
where the time goes in v1:
time: 2750 us; the launch traced here: 2740 us
  waiting for transfers between devices  1280 us (47%)
  local copies, waits for them, and re-layouts  638 us (23%)
  other arithmetic  397 us (14%)
  matrix products  359 us (13%)
  blocking collectives  39.9 us (1%)
    reduce_scatter x16, waiting for transfers between devices, backward_step(): lax.psum_scatter(terms.astype(jnp.bfloat16), 'mp', scatter_dimension=2, t...  633 us
    all_gather x16, waiting for transfers between devices, forward_step(): whole = lax.all_gather(hidden, 'mp', axis=2, tiled=True)  448 us
    div x96, local copies, waits for them, and re-layouts, forward_step(): jax.nn.sigmoid(x)  173 us
    div x16, other arithmetic, forward_step(): jax.nn.sigmoid(x)  170 us
    reduce_scatter x1, waiting for transfers between devices, per_device(): lax.psum_scatter(rec_grad.astype(jnp.bfloat16), 'seq', scatter_dimension=...  142 us
    tanh x16, other arithmetic, forward_step(): cell_gate = jnp.tanh(cell_pre)  133 us
    dot_general x16, matrix products, backward_step(): jnp.einsum('dbc,dhc->dbh', grad_pre, w_rec, preferred_element_type=jnp.fl...  113 us
    dynamic_update_slice x64, local copies, waits for them, and re-layouts, recurrences(): lax.scan(forward_step, (h_init, c_init), (gates_in, live_steps))  109 us
  transfers between devices with their start and end apart: 39, of which 36 were waited for; matrix products, arithmetic and copies ran while one was open for 7% of the time, Pallas kernels for 0%

profile of v1, /device:TPU:0, one launch (start us, length us, event | category | flops | bytes accessed | tf_op | source)
XLA Modules:
  0.0 2736.5 jit_solution(15774350132596363155)
XLA Ops:
  11.5 15.1 all-gather
  31.3 10.4 fusion.44
  41.7 11.9 copy.170
  54.1 10.1 convert_bitcast_fusion
  64.2 1309.4 %while.45 = (s32[]{:T(128)}, bf16[2,256,256]{2,1,0:T(8,128)(2,1)S(1)}, f32[2,256,256]{2,1,0:T(8,128)S(1)}, bf16[16,2,256,2048]{3,2,1,0:T(8,128)(2,1)}, f32[16,2,...) while((s32[]{:T(128)}, ...), condition=%wide.wide.region_1.2_spmd, body=%wide.wide.region_0.1_spmd.sunk | while | flops 2151284736 | bytes 70526840 | solution.py:80
  67.9 29.2 %all-gather.9.cloned.1.call-done = bf16[2,256,2048]{2,1,0:T(8,128)(2,1)} async-done(((bf16[2,256,256]{2,1,0:T(8,128)(2,1)}), bf16[2,256,2048]{2,1,0:T(8,128)(2,1)}) %all-gather.9.cloned.1.call-update) | async-done | bytes 2097168 | tf_op jit(solution)/shard_map/while/body/eval_jaxpr/all_gather | solution.py:67
  106.0 10.6 fusion.142
  151.0 28.1 %all-gather.9.cloned.1.call-done = bf16[2,256,2048]{2,1,0:T(8,128)(2,1)} async-done(((bf16[2,256,256]{2,1,0:T(8,128)(2,1)}), bf16[2,256,2048]{2,1,0:T(8,128)(2,1)}) %all-gather.9.cloned.1.call-update) | async-done | bytes 2097168 | tf_op jit(solution)/shard_map/while/body/eval_jaxpr/all_gather | solution.py:67
  187.9 10.6 fusion.142
  232.8 28.1 %all-gather.9.cloned.1.call-done = bf16[2,256,2048]{2,1,0:T(8,128)(2,1)} async-done(((bf16[2,256,256]{2,1,0:T(8,128)(2,1)}), bf16[2,256,2048]{2,1,0:T(8,128)(2,1)}) %all-gather.9.cloned.1.call-update) | async-done | bytes 2097168 | tf_op jit(solution)/shard_map/while/body/eval_jaxpr/all_gather | solution.py:67
  269.8 10.6 fusion.142
  314.7 27.8 %all-gather.9.cloned.1.call-done = bf16[2,256,2048]{2,1,0:T(8,128)(2,1)} async-done(((bf16[2,256,256]{2,1,0:T(8,128)(2,1)}), bf16[2,256,2048]{2,1,0:T(8,128)(2,1)}) %all-gather.9.cloned.1.call-update) | async-done | bytes 2097168 | tf_op jit(solution)/shard_map/while/body/eval_jaxpr/all_gather | solution.py:67
  351.3 10.6 fusion.142
  396.3 27.8 %all-gather.9.cloned.1.call-done = bf16[2,256,2048]{2,1,0:T(8,128)(2,1)} async-done(((bf16[2,256,256]{2,1,0:T(8,128)(2,1)}), bf16[2,256,2048]{2,1,0:T(8,128)(2,1)}) %all-gather.9.cloned.1.call-update) | async-done | bytes 2097168 | tf_op jit(solution)/shard_map/while/body/eval_jaxpr/all_gather | solution.py:67
  432.9 10.6 fusion.142
  477.9 27.8 %all-gather.9.cloned.1.call-done = bf16[2,256,2048]{2,1,0:T(8,128)(2,1)} async-done(((bf16[2,256,256]{2,1,0:T(8,128)(2,1)}), bf16[2,256,2048]{2,1,0:T(8,128)(2,1)}) %all-gather.9.cloned.1.call-update) | async-done | bytes 2097168 | tf_op jit(solution)/shard_map/while/body/eval_jaxpr/all_gather | solution.py:67
  514.6 10.6 fusion.142
  559.5 28.0 %all-gather.9.cloned.1.call-done = bf16[2,256,2048]{2,1,0:T(8,128)(2,1)} async-done(((bf16[2,256,256]{2,1,0:T(8,128)(2,1)}), bf16[2,256,2048]{2,1,0:T(8,128)(2,1)}) %all-gather.9.cloned.1.call-update) | async-done | bytes 2097168 | tf_op jit(solution)/shard_map/while/body/eval_jaxpr/all_gather | solution.py:67
  596.4 10.6 fusion.142
  641.3 28.1 %all-gather.9.cloned.1.call-done = bf16[2,256,2048]{2,1,0:T(8,128)(2,1)} async-done(((bf16[2,256,256]{2,1,0:T(8,128)(2,1)}), bf16[2,256,2048]{2,1,0:T(8,128)(2,1)}) %all-gather.9.cloned.1.call-update) | async-done | bytes 2097168 | tf_op jit(solution)/shard_map/while/body/eval_jaxpr/all_gather | solution.py:67
  678.3 10.6 fusion.142
  723.2 28.1 %all-gather.9.cloned.1.call-done = bf16[2,256,2048]{2,1,0:T(8,128)(2,1)} async-done(((bf16[2,256,256]{2,1,0:T(8,128)(2,1)}), bf16[2,256,2048]{2,1,0:T(8,128)(2,1)}) %all-gather.9.cloned.1.call-update) | async-done | bytes 2097168 | tf_op jit(solution)/shard_map/while/body/eval_jaxpr/all_gather | solution.py:67
  760.2 10.6 fusion.142
  805.1 27.7 %all-gather.9.cloned.1.call-done = bf16[2,256,2048]{2,1,0:T(8,128)(2,1)} async-done(((bf16[2,256,256]{2,1,0:T(8,128)(2,1)}), bf16[2,256,2048]{2,1,0:T(8,128)(2,1)}) %all-gather.9.cloned.1.call-update) | async-done | bytes 2097168 | tf_op jit(solution)/shard_map/while/body/eval_jaxpr/all_gather | solution.py:67
  841.8 10.6 fusion.142
  886.6 28.1 %all-gather.9.cloned.1.call-done = bf16[2,256,2048]{2,1,0:T(8,128)(2,1)} async-done(((bf16[2,256,256]{2,1,0:T(8,128)(2,1)}), bf16[2,256,2048]{2,1,0:T(8,128)(2,1)}) %all-gather.9.cloned.1.call-update) | async-done | bytes 2097168 | tf_op jit(solution)/shard_map/while/body/eval_jaxpr/all_gather | solution.py:67
  923.6 10.6 fusion.142
  968.5 27.8 %all-gather.9.cloned.1.call-done = bf16[2,256,2048]{2,1,0:T(8,128)(2,1)} async-done(((bf16[2,256,256]{2,1,0:T(8,128)(2,1)}), bf16[2,256,2048]{2,1,0:T(8,128)(2,1)}) %all-gather.9.cloned.1.call-update) | async-done | bytes 2097168 | tf_op jit(solution)/shard_map/while/body/eval_jaxpr/all_gather | solution.py:67
  1005.2 10.6 fusion.142
  1050.1 28.0 %all-gather.9.cloned.1.call-done = bf16[2,256,2048]{2,1,0:T(8,128)(2,1)} async-done(((bf16[2,256,256]{2,1,0:T(8,128)(2,1)}), bf16[2,256,2048]{2,1,0:T(8,128)(2,1)}) %all-gather.9.cloned.1.call-update) | async-done | bytes 2097168 | tf_op jit(solution)/shard_map/while/body/eval_jaxpr/all_gather | solution.py:67
  1087.0 10.6 fusion.142
  1132.0 27.8 %all-gather.9.cloned.1.call-done = bf16[2,256,2048]{2,1,0:T(8,128)(2,1)} async-done(((bf16[2,256,256]{2,1,0:T(8,128)(2,1)}), bf16[2,256,2048]{2,1,0:T(8,128)(2,1)}) %all-gather.9.cloned.1.call-update) | async-done | bytes 2097168 | tf_op jit(solution)/shard_map/while/body/eval_jaxpr/all_gather | solution.py:67
  1168.6 10.6 fusion.142
  1213.6 27.8 %all-gather.9.cloned.1.call-done = bf16[2,256,2048]{2,1,0:T(8,128)(2,1)} async-done(((bf16[2,256,256]{2,1,0:T(8,128)(2,1)}), bf16[2,256,2048]{2,1,0:T(8,128)(2,1)}) %all-gather.9.cloned.1.call-update) | async-done | bytes 2097168 | tf_op jit(solution)/shard_map/while/body/eval_jaxpr/all_gather | solution.py:67
  1250.2 10.6 fusion.142
  1295.1 27.7 %all-gather.9.cloned.1.call-done = bf16[2,256,2048]{2,1,0:T(8,128)(2,1)} async-done(((bf16[2,256,256]{2,1,0:T(8,128)(2,1)}), bf16[2,256,2048]{2,1,0:T(8,128)(2,1)}) %all-gather.9.cloned.1.call-update) | async-done | bytes 2097168 | tf_op jit(solution)/shard_map/while/body/eval_jaxpr/all_gather | solution.py:67
  1331.8 10.6 fusion.142
  1378.8 23.3 copy.172
  1402.1 20.9 slice.40
  1423.8 12.0 all-gather.7.cloned.1.call-done
  1435.9 15.9 bitcast_reduce_fusion
  1469.3 955.0 %while.44 = (s32[]{:T(128)}, f32[2,256,256]{1,2,0:T(8,128)}, f32[2,256,256]{1,2,0:T(8,128)}, bf16[16,2,256,1024]{3,2,1,0:T(8,128)(2,1)}, pred[16,2,256,1]{2,1,3,...) while((s32[]{:T(128)}, f32[2,256,256]{1,2,0:T(8,128)}, ...), condition=%wide.region_11.12_spmd.clone, body=%wide.region_9.11_spmd.clone.sunk | while | flops 2227306496 | bytes 52475628 | solution.py:138
  1487.5 39.6 %reduce-scatter.11.cloned.1.call-done = bf16[2,256,256]{1,2,0:T(8,128)(2,1)} async-done(((bf16[2,256,2048]{1,2,0:T(8,128)(2,1)}), bf16[2,256,256]{1,2,0:T(8,128)(2,1)}) %reduce-scatter.11.cloned.1.call-update) | async-done | bytes 262160 | tf_op jit(solution)/shard_map/while/body/eval_jaxpr/reduce_scatter | solution.py:132
  1547.2 39.5 %reduce-scatter.11.cloned.1.call-done = bf16[2,256,256]{1,2,0:T(8,128)(2,1)} async-done(((bf16[2,256,2048]{1,2,0:T(8,128)(2,1)}), bf16[2,256,256]{1,2,0:T(8,128)(2,1)}) %reduce-scatter.11.cloned.1.call-update) | async-done | bytes 262160 | tf_op jit(solution)/shard_map/while/body/eval_jaxpr/reduce_scatter | solution.py:132
  1606.9 39.6 %reduce-scatter.11.cloned.1.call-done = bf16[2,256,256]{1,2,0:T(8,128)(2,1)} async-done(((bf16[2,256,2048]{1,2,0:T(8,128)(2,1)}), bf16[2,256,256]{1,2,0:T(8,128)(2,1)}) %reduce-scatter.11.cloned.1.call-update) | async-done | bytes 262160 | tf_op jit(solution)/shard_map/while/body/eval_jaxpr/reduce_scatter | solution.py:132
  1666.6 39.6 %reduce-scatter.11.cloned.1.call-done = bf16[2,256,256]{1,2,0:T(8,128)(2,1)} async-done(((bf16[2,256,2048]{1,2,0:T(8,128)(2,1)}), bf16[2,256,256]{1,2,0:T(8,128)(2,1)}) %reduce-scatter.11.cloned.1.call-update) | async-done | bytes 262160 | tf_op jit(solution)/shard_map/while/body/eval_jaxpr/reduce_scatter | solution.py:132
  1726.2 39.6 %reduce-scatter.11.cloned.1.call-done = bf16[2,256,256]{1,2,0:T(8,128)(2,1)} async-done(((bf16[2,256,2048]{1,2,0:T(8,128)(2,1)}), bf16[2,256,256]{1,2,0:T(8,128)(2,1)}) %reduce-scatter.11.cloned.1.call-update) | async-done | bytes 262160 | tf_op jit(solution)/shard_map/while/body/eval_jaxpr/reduce_scatter | solution.py:132
  1785.9 39.6 %reduce-scatter.11.cloned.1.call-done = bf16[2,256,256]{1,2,0:T(8,128)(2,1)} async-done(((bf16[2,256,2048]{1,2,0:T(8,128)(2,1)}), bf16[2,256,256]{1,2,0:T(8,128)(2,1)}) %reduce-scatter.11.cloned.1.call-update) | async-done | bytes 262160 | tf_op jit(solution)/shard_map/while/body/eval_jaxpr/reduce_scatter | solution.py:132
  1845.7 39.5 %reduce-scatter.11.cloned.1.call-done = bf16[2,256,256]{1,2,0:T(8,128)(2,1)} async-done(((bf16[2,256,2048]{1,2,0:T(8,128)(2,1)}), bf16[2,256,256]{1,2,0:T(8,128)(2,1)}) %reduce-scatter.11.cloned.1.call-update) | async-done | bytes 262160 | tf_op jit(solution)/shard_map/while/body/eval_jaxpr/reduce_scatter | solution.py:132
  1905.3 39.6 %reduce-scatter.11.cloned.1.call-done = bf16[2,256,256]{1,2,0:T(8,128)(2,1)} async-done(((bf16[2,256,2048]{1,2,0:T(8,128)(2,1)}), bf16[2,256,256]{1,2,0:T(8,128)(2,1)}) %reduce-scatter.11.cloned.1.call-update) | async-done | bytes 262160 | tf_op jit(solution)/shard_map/while/body/eval_jaxpr/reduce_scatter | solution.py:132
  1965.0 39.6 %reduce-scatter.11.cloned.1.call-done = bf16[2,256,256]{1,2,0:T(8,128)(2,1)} async-done(((bf16[2,256,2048]{1,2,0:T(8,128)(2,1)}), bf16[2,256,256]{1,2,0:T(8,128)(2,1)}) %reduce-scatter.11.cloned.1.call-update) | async-done | bytes 262160 | tf_op jit(solution)/shard_map/while/body/eval_jaxpr/reduce_scatter | solution.py:132
  2024.7 39.6 %reduce-scatter.11.cloned.1.call-done = bf16[2,256,256]{1,2,0:T(8,128)(2,1)} async-done(((bf16[2,256,2048]{1,2,0:T(8,128)(2,1)}), bf16[2,256,256]{1,2,0:T(8,128)(2,1)}) %reduce-scatter.11.cloned.1.call-update) | async-done | bytes 262160 | tf_op jit(solution)/shard_map/while/body/eval_jaxpr/reduce_scatter | solution.py:132
  2084.4 39.6 %reduce-scatter.11.cloned.1.call-done = bf16[2,256,256]{1,2,0:T(8,128)(2,1)} async-done(((bf16[2,256,2048]{1,2,0:T(8,128)(2,1)}), bf16[2,256,256]{1,2,0:T(8,128)(2,1)}) %reduce-scatter.11.cloned.1.call-update) | async-done | bytes 262160 | tf_op jit(solution)/shard_map/while/body/eval_jaxpr/reduce_scatter | solution.py:132
  2144.1 39.6 %reduce-scatter.11.cloned.1.call-done = bf16[2,256,256]{1,2,0:T(8,128)(2,1)} async-done(((bf16[2,256,2048]{1,2,0:T(8,128)(2,1)}), bf16[2,256,256]{1,2,0:T(8,128)(2,1)}) %reduce-scatter.11.cloned.1.call-update) | async-done | bytes 262160 | tf_op jit(solution)/shard_map/while/body/eval_jaxpr/reduce_scatter | solution.py:132
  2203.8 39.5 %reduce-scatter.11.cloned.1.call-done = bf16[2,256,256]{1,2,0:T(8,128)(2,1)} async-done(((bf16[2,256,2048]{1,2,0:T(8,128)(2,1)}), bf16[2,256,256]{1,2,0:T(8,128)(2,1)}) %reduce-scatter.11.cloned.1.call-update) | async-done | bytes 262160 | tf_op jit(solution)/shard_map/while/body/eval_jaxpr/reduce_scatter | solution.py:132
  2263.5 39.6 %reduce-scatter.11.cloned.1.call-done = bf16[2,256,256]{1,2,0:T(8,128)(2,1)} async-done(((bf16[2,256,2048]{1,2,0:T(8,128)(2,1)}), bf16[2,256,256]{1,2,0:T(8,128)(2,1)}) %reduce-scatter.11.cloned.1.call-update) | async-done | bytes 262160 | tf_op jit(solution)/shard_map/while/body/eval_jaxpr/reduce_scatter | solution.py:132
  2323.2 39.5 %reduce-scatter.11.cloned.1.call-done = bf16[2,256,256]{1,2,0:T(8,128)(2,1)} async-done(((bf16[2,256,2048]{1,2,0:T(8,128)(2,1)}), bf16[2,256,256]{1,2,0:T(8,128)(2,1)}) %reduce-scatter.11.cloned.1.call-update) | async-done | bytes 262160 | tf_op jit(solution)/shard_map/while/body/eval_jaxpr/reduce_scatter | solution.py:132
  2382.9 39.6 %reduce-scatter.11.cloned.1.call-done = bf16[2,256,256]{1,2,0:T(8,128)(2,1)} async-done(((bf16[2,256,2048]{1,2,0:T(8,128)(2,1)}), bf16[2,256,256]{1,2,0:T(8,128)(2,1)}) %reduce-scatter.11.cloned.1.call-update) | async-done | bytes 262160 | tf_op jit(solution)/shard_map/while/body/eval_jaxpr/reduce_scatter | solution.py:132
  2441.0 29.4 %all-reduce.5.cloned.1.call-done = f32[2,275,100]{2,1,0:T(8,128)} async-done(((f32[2,275,100]{2,1,0:T(8,128)}), f32[2,275,100]{2,1,0:T(8,128)}) %all-reduce.5.cloned.1.call-update) | async-done | bytes 220016 | tf_op jit(solution)/shard_map/psum | solution.py:214
  2481.1 42.9 %bitcast_convert_fusion = bf16[2,2048,1024]{2,1,0:T(8,128)(2,1)} fusion(bf16[16,2,256,2048]{3,2,1,0:T(8,128)(2,1)} %get-tuple-element.342, bf16[16,2,256,1024]{3,2,1,0:T(8,128)(2,1)} %get-tuple-element.351), kind=kOutput, calls=%fused_computation.74 | convolution fusion | flops 34363932672 | bytes 58720256 | tf_op jit(solution)/shard_map/sdbh,sdbc->dhc/dot_general | solution.py:141
  2526.4 11.1 all-reduce.1
  2537.5 13.8 all-reduce
  2558.3 13.2 reduce-scatter.5.cloned.1.call-done
  2575.0 141.9 %reduce-scatter.7.cloned.1.call-done = bf16[2,512,1024]{2,1,0:T(8,128)(2,1)} async-done(((bf16[2,2048,1024]{2,1,0:T(8,128)(2,1)}), bf16[2,512,1024]{2,1,0:T(8,128)(2,1)}) %reduce-scatter.7.cloned.1.call-update) | async-done | bytes 2097168 | tf_op jit(solution)/shard_map/reduce_scatter | solution.py:206
  (961 shorter events, 1090.1 us)
Async XLA Ops:
  64.2 1312.0 %copy-start.1 = (s32[1024]{0:T(1024)S(1)}, s32[1024]{0:T(1024)}, u32[]{:S(2)}) copy-start(s32[1024]{0:T(1024)} %param.16) | copy-start | bytes 12292
  64.5 32.6 %all-gather.9.cloned.1.call-start = ((), (), s32[]{:S(2)}) async-start(), calls=%async_computation.12 | async-start | bytes 2359296 | tf_op jit(solution)/shard_map/while/body/eval_jaxpr/all_gather | solution.py:67
  106.0 38.3 %copy-start.3 = (f32[2,256,256]{2,1,0:T(8,128)S(1)}, f32[2,256,256]{2,1,0:T(8,128)}, u32[]{:S(2)}) copy-start(f32[2,256,256]{2,1,0:T(8,128)} %copy-done.2) | copy-start | bytes 1572868 | tf_op jit(solution)/shard_map/while
  106.0 38.3 %copy-start.6 = (bf16[2,256,256]{2,1,0:T(8,128)(2,1)S(1)}, bf16[2,256,256]{2,1,0:T(8,128)(2,1)}, u32[]{:S(2)}) copy-start(bf16[2,256,256]{2,1,0:T(8,128)(2,1)} %copy-done.5) | copy-start | bytes 786436 | tf_op jit(solution)/shard_map/while
  147.5 31.5 %all-gather.9.cloned.1.call-start = ((), (), s32[]{:S(2)}) async-start(), calls=%async_computation.12 | async-start | bytes 2359296 | tf_op jit(solution)/shard_map/while/body/eval_jaxpr/all_gather | solution.py:67
  187.9 38.2 %copy-start.3 = (f32[2,256,256]{2,1,0:T(8,128)S(1)}, f32[2,256,256]{2,1,0:T(8,128)}, u32[]{:S(2)}) copy-start(f32[2,256,256]{2,1,0:T(8,128)} %copy-done.2) | copy-start | bytes 1572868 | tf_op jit(solution)/shard_map/while
  187.9 38.2 %copy-start.6 = (bf16[2,256,256]{2,1,0:T(8,128)(2,1)S(1)}, bf16[2,256,256]{2,1,0:T(8,128)(2,1)}, u32[]{:S(2)}) copy-start(bf16[2,256,256]{2,1,0:T(8,128)(2,1)} %copy-done.5) | copy-start | bytes 786436 | tf_op jit(solution)/shard_map/while
  229.4 31.5 %all-gather.9.cloned.1.call-start = ((), (), s32[]{:S(2)}) async-start(), calls=%async_computation.12 | async-start | bytes 2359296 | tf_op jit(solution)/shard_map/while/body/eval_jaxpr/all_gather | solution.py:67
  311.2 31.2 %all-gather.9.cloned.1.call-start = ((), (), s32[]{:S(2)}) async-start(), calls=%async_computation.12 | async-start | bytes 2359296 | tf_op jit(solution)/shard_map/while/body/eval_jaxpr/all_gather | solution.py:67
  351.3 38.3 %copy-start.3 = (f32[2,256,256]{2,1,0:T(8,128)S(1)}, f32[2,256,256]{2,1,0:T(8,128)}, u32[]{:S(2)}) copy-start(f32[2,256,256]{2,1,0:T(8,128)} %copy-done.2) | copy-start | bytes 1572868 | tf_op jit(solution)/shard_map/while
  351.3 38.3 %copy-start.6 = (bf16[2,256,256]{2,1,0:T(8,128)(2,1)S(1)}, bf16[2,256,256]{2,1,0:T(8,128)(2,1)}, u32[]{:S(2)}) copy-start(bf16[2,256,256]{2,1,0:T(8,128)(2,1)} %copy-done.5) | copy-start | bytes 786436 | tf_op jit(solution)/shard_map/while
  392.8 31.2 %all-gather.9.cloned.1.call-start = ((), (), s32[]{:S(2)}) async-start(), calls=%async_computation.12 | async-start | bytes 2359296 | tf_op jit(solution)/shard_map/while/body/eval_jaxpr/all_gather | solution.py:67
  432.9 38.3 %copy-start.3 = (f32[2,256,256]{2,1,0:T(8,128)S(1)}, f32[2,256,256]{2,1,0:T(8,128)}, u32[]{:S(2)}) copy-start(f32[2,256,256]{2,1,0:T(8,128)} %copy-done.2) | copy-start | bytes 1572868 | tf_op jit(solution)/shard_map/while
  432.9 38.3 %copy-start.6 = (bf16[2,256,256]{2,1,0:T(8,128)(2,1)S(1)}, bf16[2,256,256]{2,1,0:T(8,128)(2,1)}, u32[]{:S(2)}) copy-start(bf16[2,256,256]{2,1,0:T(8,128)(2,1)} %copy-done.5) | copy-start | bytes 786436 | tf_op jit(solution)/shard_map/while
  474.4 31.2 %all-gather.9.cloned.1.call-start = ((), (), s32[]{:S(2)}) async-start(), calls=%async_computation.12 | async-start | bytes 2359296 | tf_op jit(solution)/shard_map/while/body/eval_jaxpr/all_gather | solution.py:67
  514.5 38.2 %copy-start.3 = (f32[2,256,256]{2,1,0:T(8,128)S(1)}, f32[2,256,256]{2,1,0:T(8,128)}, u32[]{:S(2)}) copy-start(f32[2,256,256]{2,1,0:T(8,128)} %copy-done.2) | copy-start | bytes 1572868 | tf_op jit(solution)/shard_map/while
  514.5 38.2 %copy-start.6 = (bf16[2,256,256]{2,1,0:T(8,128)(2,1)S(1)}, bf16[2,256,256]{2,1,0:T(8,128)(2,1)}, u32[]{:S(2)}) copy-start(bf16[2,256,256]{2,1,0:T(8,128)(2,1)} %copy-done.5) | copy-start | bytes 786436 | tf_op jit(solution)/shard_map/while
  556.0 31.5 %all-gather.9.cloned.1.call-start = ((), (), s32[]{:S(2)}) async-start(), calls=%async_computation.12 | async-start | bytes 2359296 | tf_op jit(solution)/shard_map/while/body/eval_jaxpr/all_gather | solution.py:67
  637.9 31.5 %all-gather.9.cloned.1.call-start = ((), (), s32[]{:S(2)}) async-start(), calls=%async_computation.12 | async-start | bytes 2359296 | tf_op jit(solution)/shard_map/while/body/eval_jaxpr/all_gather | solution.py:67
  678.3 38.2 %copy-start.3 = (f32[2,256,256]{2,1,0:T(8,128)S(1)}, f32[2,256,256]{2,1,0:T(8,128)}, u32[]{:S(2)}) copy-start(f32[2,256,256]{2,1,0:T(8,128)} %copy-done.2) | copy-start | bytes 1572868 | tf_op jit(solution)/shard_map/while
  678.3 38.2 %copy-start.6 = (bf16[2,256,256]{2,1,0:T(8,128)(2,1)S(1)}, bf16[2,256,256]{2,1,0:T(8,128)(2,1)}, u32[]{:S(2)}) copy-start(bf16[2,256,256]{2,1,0:T(8,128)(2,1)} %copy-done.5) | copy-start | bytes 786436 | tf_op jit(solution)/shard_map/while
  719.7 31.5 %all-gather.9.cloned.1.call-start = ((), (), s32[]{:S(2)}) async-start(), calls=%async_computation.12 | async-start | bytes 2359296 | tf_op jit(solution)/shard_map/while/body/eval_jaxpr/all_gather | solution.py:67
  760.1 38.3 %copy-start.3 = (f32[2,256,256]{2,1,0:T(8,128)S(1)}, f32[2,256,256]{2,1,0:T(8,128)}, u32[]{:S(2)}) copy-start(f32[2,256,256]{2,1,0:T(8,128)} %copy-done.2) | copy-start | bytes 1572868 | tf_op jit(solution)/shard_map/while
  760.1 38.3 %copy-start.6 = (bf16[2,256,256]{2,1,0:T(8,128)(2,1)S(1)}, bf16[2,256,256]{2,1,0:T(8,128)(2,1)}, u32[]{:S(2)}) copy-start(bf16[2,256,256]{2,1,0:T(8,128)(2,1)} %copy-done.5) | copy-start | bytes 786436 | tf_op jit(solution)/shard_map/while
  801.7 31.2 %all-gather.9.cloned.1.call-start = ((), (), s32[]{:S(2)}) async-start(), calls=%async_computation.12 | async-start | bytes 2359296 | tf_op jit(solution)/shard_map/while/body/eval_jaxpr/all_gather | solution.py:67
  841.8 38.3 %copy-start.3 = (f32[2,256,256]{2,1,0:T(8,128)S(1)}, f32[2,256,256]{2,1,0:T(8,128)}, u32[]{:S(2)}) copy-start(f32[2,256,256]{2,1,0:T(8,128)} %copy-done.2) | copy-start | bytes 1572868 | tf_op jit(solution)/shard_map/while
  841.8 38.3 %copy-start.6 = (bf16[2,256,256]{2,1,0:T(8,128)(2,1)S(1)}, bf16[2,256,256]{2,1,0:T(8,128)(2,1)}, u32[]{:S(2)}) copy-start(bf16[2,256,256]{2,1,0:T(8,128)(2,1)} %copy-done.5) | copy-start | bytes 786436 | tf_op jit(solution)/shard_map/while
  883.2 31.5 %all-gather.9.cloned.1.call-start = ((), (), s32[]{:S(2)}) async-start(), calls=%async_computation.12 | async-start | bytes 2359296 | tf_op jit(solution)/shard_map/while/body/eval_jaxpr/all_gather | solution.py:67
  965.1 31.2 %all-gather.9.cloned.1.call-start = ((), (), s32[]{:S(2)}) async-start(), calls=%async_computation.12 | async-start | bytes 2359296 | tf_op jit(solution)/shard_map/while/body/eval_jaxpr/all_gather | solution.py:67
  1046.6 31.5 %all-gather.9.cloned.1.call-start = ((), (), s32[]{:S(2)}) async-start(), calls=%async_computation.12 | async-start | bytes 2359296 | tf_op jit(solution)/shard_map/while/body/eval_jaxpr/all_gather | solution.py:67
  1087.0 38.3 %copy-start.3 = (f32[2,256,256]{2,1,0:T(8,128)S(1)}, f32[2,256,256]{2,1,0:T(8,128)}, u32[]{:S(2)}) copy-start(f32[2,256,256]{2,1,0:T(8,128)} %copy-done.2) | copy-start | bytes 1572868 | tf_op jit(solution)/shard_map/while
  1087.0 38.3 %copy-start.6 = (bf16[2,256,256]{2,1,0:T(8,128)(2,1)S(1)}, bf16[2,256,256]{2,1,0:T(8,128)(2,1)}, u32[]{:S(2)}) copy-start(bf16[2,256,256]{2,1,0:T(8,128)(2,1)} %copy-done.5) | copy-start | bytes 786436 | tf_op jit(solution)/shard_map/while
  1128.5 31.2 %all-gather.9.cloned.1.call-start = ((), (), s32[]{:S(2)}) async-start(), calls=%async_computation.12 | async-start | bytes 2359296 | tf_op jit(solution)/shard_map/while/body/eval_jaxpr/all_gather | solution.py:67
  1168.6 38.3 %copy-start.3 = (f32[2,256,256]{2,1,0:T(8,128)S(1)}, f32[2,256,256]{2,1,0:T(8,128)}, u32[]{:S(2)}) copy-start(f32[2,256,256]{2,1,0:T(8,128)} %copy-done.2) | copy-start | bytes 1572868 | tf_op jit(solution)/shard_map/while
  1168.6 38.3 %copy-start.6 = (bf16[2,256,256]{2,1,0:T(8,128)(2,1)S(1)}, bf16[2,256,256]{2,1,0:T(8,128)(2,1)}, u32[]{:S(2)}) copy-start(bf16[2,256,256]{2,1,0:T(8,128)(2,1)} %copy-done.5) | copy-start | bytes 786436 | tf_op jit(solution)/shard_map/while
  1210.1 31.2 %all-gather.9.cloned.1.call-start = ((), (), s32[]{:S(2)}) async-start(), calls=%async_computation.12 | async-start | bytes 2359296 | tf_op jit(solution)/shard_map/while/body/eval_jaxpr/all_gather | solution.py:67
  1291.7 31.2 %all-gather.9.cloned.1.call-start = ((), (), s32[]{:S(2)}) async-start(), calls=%async_computation.12 | async-start | bytes 2359296 | tf_op jit(solution)/shard_map/while/body/eval_jaxpr/all_gather | solution.py:67
  1331.8 38.3 %copy-start.3 = (f32[2,256,256]{2,1,0:T(8,128)S(1)}, f32[2,256,256]{2,1,0:T(8,128)}, u32[]{:S(2)}) copy-start(f32[2,256,256]{2,1,0:T(8,128)} %copy-done.2) | copy-start | bytes 1572868 | tf_op jit(solution)/shard_map/while
  1331.8 38.3 %copy-start.6 = (bf16[2,256,256]{2,1,0:T(8,128)(2,1)S(1)}, bf16[2,256,256]{2,1,0:T(8,128)(2,1)}, u32[]{:S(2)}) copy-start(bf16[2,256,256]{2,1,0:T(8,128)(2,1)} %copy-done.5) | copy-start | bytes 786436 | tf_op jit(solution)/shard_map/while
  1373.7 50.2 %all-gather.5.cloned.1.call-start = ((), (), s32[]{:S(2)}) async-start(), calls=%async_computation.4 | async-start | bytes 2359296 | tf_op jit(solution)/shard_map/all_gather | solution.py:83
  1374.4 61.5 %all-gather.7.cloned.1.call-start = ((), (), s32[]{:S(2)}) async-start(), calls=%async_computation.5 | async-start | bytes 2580480 | tf_op jit(solution)/shard_map/all_gather | solution.py:165
  1469.3 955.0 %copy-start.17 = (s32[16,2,256]{2,0,1:T(8,128)S(1)}, s32[16,2,256]{2,0,1:T(8,128)}, u32[]{:S(2)}) copy-start(s32[16,2,256]{2,0,1:T(8,128)} %copy-done.16) | copy-start | bytes 98308
  1469.4 57.6 %reduce-scatter.11.cloned.1.call-start = ((), (), s32[]{:S(2)}) async-start(), calls=%async_computation.11 | async-start | bytes 2359296 | tf_op jit(solution)/shard_map/while/body/eval_jaxpr/reduce_scatter | solution.py:132
  1528.9 57.9 %reduce-scatter.11.cloned.1.call-start = ((), (), s32[]{:S(2)}) async-start(), calls=%async_computation.11 | async-start | bytes 2359296 | tf_op jit(solution)/shard_map/while/body/eval_jaxpr/reduce_scatter | solution.py:132
  1588.6 57.9 %reduce-scatter.11.cloned.1.call-start = ((), (), s32[]{:S(2)}) async-start(), calls=%async_computation.11 | async-start | bytes 2359296 | tf_op jit(solution)/shard_map/while/body/eval_jaxpr/reduce_scatter | solution.py:132
  1648.3 57.9 %reduce-scatter.11.cloned.1.call-start = ((), (), s32[]{:S(2)}) async-start(), calls=%async_computation.11 | async-start | bytes 2359296 | tf_op jit(solution)/shard_map/while/body/eval_jaxpr/reduce_scatter | solution.py:132
  1707.9 57.9 %reduce-scatter.11.cloned.1.call-start = ((), (), s32[]{:S(2)}) async-start(), calls=%async_computation.11 | async-start | bytes 2359296 | tf_op jit(solution)/shard_map/while/body/eval_jaxpr/reduce_scatter | solution.py:132
  1767.6 57.9 %reduce-scatter.11.cloned.1.call-start = ((), (), s32[]{:S(2)}) async-start(), calls=%async_computation.11 | async-start | bytes 2359296 | tf_op jit(solution)/shard_map/while/body/eval_jaxpr/reduce_scatter | solution.py:132
  1827.3 57.9 %reduce-scatter.11.cloned.1.call-start = ((), (), s32[]{:S(2)}) async-start(), calls=%async_computation.11 | async-start | bytes 2359296 | tf_op jit(solution)/shard_map/while/body/eval_jaxpr/reduce_scatter | solution.py:132
  1887.0 57.9 %reduce-scatter.11.cloned.1.call-start = ((), (), s32[]{:S(2)}) async-start(), calls=%async_computation.11 | async-start | bytes 2359296 | tf_op jit(solution)/shard_map/while/body/eval_jaxpr/reduce_scatter | solution.py:132
  1946.7 57.9 %reduce-scatter.11.cloned.1.call-start = ((), (), s32[]{:S(2)}) async-start(), calls=%async_computation.11 | async-start | bytes 2359296 | tf_op jit(solution)/shard_map/while/body/eval_jaxpr/reduce_scatter | solution.py:132
  2006.4 57.9 %reduce-scatter.11.cloned.1.call-start = ((), (), s32[]{:S(2)}) async-start(), calls=%async_computation.11 | async-start | bytes 2359296 | tf_op jit(solution)/shard_map/while/body/eval_jaxpr/reduce_scatter | solution.py:132
  2066.1 57.9 %reduce-scatter.11.cloned.1.call-start = ((), (), s32[]{:S(2)}) async-start(), calls=%async_computation.11 | async-start | bytes 2359296 | tf_op jit(solution)/shard_map/while/body/eval_jaxpr/reduce_scatter | solution.py:132
  2125.8 57.9 %reduce-scatter.11.cloned.1.call-start = ((), (), s32[]{:S(2)}) async-start(), calls=%async_computation.11 | async-start | bytes 2359296 | tf_op jit(solution)/shard_map/while/body/eval_jaxpr/reduce_scatter | solution.py:132
  2185.5 57.9 %reduce-scatter.11.cloned.1.call-start = ((), (), s32[]{:S(2)}) async-start(), calls=%async_computation.11 | async-start | bytes 2359296 | tf_op jit(solution)/shard_map/while/body/eval_jaxpr/reduce_scatter | solution.py:132
  2245.2 57.9 %reduce-scatter.11.cloned.1.call-start = ((), (), s32[]{:S(2)}) async-start(), calls=%async_computation.11 | async-start | bytes 2359296 | tf_op jit(solution)/shard_map/while/body/eval_jaxpr/reduce_scatter | solution.py:132
  2304.8 57.9 %reduce-scatter.11.cloned.1.call-start = ((), (), s32[]{:S(2)}) async-start(), calls=%async_computation.11 | async-start | bytes 2359296 | tf_op jit(solution)/shard_map/while/body/eval_jaxpr/reduce_scatter | solution.py:132
  2364.6 57.9 %reduce-scatter.11.cloned.1.call-start = ((), (), s32[]{:S(2)}) async-start(), calls=%async_computation.11 | async-start | bytes 2359296 | tf_op jit(solution)/shard_map/while/body/eval_jaxpr/reduce_scatter | solution.py:132
  2424.3 46.1 %all-reduce.5.cloned.1.call-start = ((), (), s32[]{:S(2)}) async-start(), calls=%async_computation.6 | async-start | bytes 573440 | tf_op jit(solution)/shard_map/psum | solution.py:214
  2434.8 120.1 %all-reduce.7.cloned.1.call-start = ((), (), s32[]{:S(2)}) async-start(), calls=%async_computation.7 | async-start | bytes 573440 | tf_op jit(solution)/shard_map/psum | solution.py:213
  2470.4 86.4 %reduce-scatter.9.cloned.1.call-start = ((), (), s32[]{:S(2)}) async-start(), calls=%async_computation.10 | async-start | bytes 491520 | tf_op jit(solution)/shard_map/reduce_scatter | solution.py:210
  2478.0 93.6 %reduce-scatter.5.cloned.1.call-start = ((), (), s32[]{:S(2)}) async-start(), calls=%async_computation.8 | async-start | bytes 655360 | tf_op jit(solution)/shard_map/reduce_scatter | solution.py:209
  2481.0 235.9 %reduce-scatter.7.cloned.1.call-start = ((), (), s32[]{:S(2)}) async-start(), calls=%async_computation.9 | async-start | bytes 10485760 | tf_op jit(solution)/shard_map/reduce_scatter | solution.py:206
  2524.0 192.9 %copy-start.24 = (s32[512]{0:T(512)S(1)}, s32[512]{0:T(512)}, u32[]{:S(2)}) copy-start(s32[512]{0:T(512)} %copy-done.23) | copy-start | bytes 6148
  (76 other events, 1613.1 us)
Sparse Core Ops, SparseCore 0:
  67.8 29.3 all-gather.8
  150.8 28.1 all-gather.8
  232.6 28.1 all-gather.8
  314.2 28.1 all-gather.8
  395.8 28.1 all-gather.8
  477.4 28.1 all-gather.8
  559.3 28.1 all-gather.8
  641.2 28.1 all-gather.8
  723.0 28.1 all-gather.8
  804.6 28.1 all-gather.8
  886.5 28.1 all-gather.8
  968.0 28.1 all-gather.8
  1049.9 28.1 all-gather.8
  1131.5 28.1 all-gather.8
  1213.1 28.1 all-gather.8
  1294.6 28.1 all-gather.8
  1485.8 41.2 reduce-scatter.10
  1545.5 41.2 reduce-scatter.10
  1605.2 41.2 reduce-scatter.10
  1664.9 41.2 reduce-scatter.10
  1724.6 41.2 reduce-scatter.10
  1784.2 41.2 reduce-scatter.10
  1843.9 41.2 reduce-scatter.10
  1903.6 41.2 reduce-scatter.10
  1963.3 41.2 reduce-scatter.10
  2023.0 41.2 reduce-scatter.10
  2082.7 41.2 reduce-scatter.10
  2142.4 41.2 reduce-scatter.10
  2202.1 41.2 reduce-scatter.10
  2261.8 41.2 reduce-scatter.10
  2321.5 41.2 reduce-scatter.10
  2381.2 41.2 reduce-scatter.10
Sparse Core Ops, SparseCore 1:
  1376.6 28.0 all-gather.4
  1406.9 28.9 all-gather.6
  2434.9 35.4 all-reduce.4
  2473.5 51.8 all-reduce.6
  2527.7 21.2 reduce-scatter.8
  2551.9 19.6 reduce-scatter.4
  2573.9 142.9 reduce-scatter.6
